TPU v7x, 32 devices: a whole 2x2x4 slice. The times are simulated.
32 devices in a mesh: dp: 16 (over z, x, core), tensor: 2 (over y).
Axes of the slice: x: 2, y: 2, z: 4, core: 2. Of those that a mesh axis runs over, the one named last changes fastest.
Arguments:
- block_input: bfloat16 [8192, 1024], P(('dp', 'tensor')), may hold values from -6 to 6
- first_layer_values: bfloat16 [8192, 1024], P('dp', 'tensor'), may hold values from -6 to 6
- segments: int32 [16, 512], P('dp'), may hold values from 0 to 1, as said below
- valid: int32 [16, 512], replicated, may hold values 0 or 1
- cotangent: bfloat16 [8192, 1024], P(('dp', 'tensor')), may hold values from -6 to 6
- teacher: bfloat16 [8192, 1024], P(('dp', 'tensor')), may hold values from -6 to 6
- layer_norm_gain: float32 [2, 1024], replicated, may hold values from 0.1 to 1.9
- layer_norm_bias: float32 [2, 1024], replicated, may hold values from -2 to 2
- lerps: float32 [7, 1024], replicated, may hold values from 0.05 to 0.95
- decay_offset: float32 [1024], replicated, may hold values from -7 to -1
- head_gain_table: float32 [3, 1024], replicated, may hold values from 0.1 to 1.9
- per_unit_shift_array: float32 [4, 1024], replicated, may hold values from -3 to 3
- lowrank_first_maps: bfloat16 [1024, 288], replicated, may hold values from -0.1875 to 0.1875
- lowrank_second_maps: bfloat16 [288, 1024], replicated, may hold values from -0.75 to 0.75
- receptance_key_value_weight: bfloat16 [3, 1024, 1024], P(None, 'dp', 'tensor'), may hold values from -0.1875 to 0.1875
- time_output_weight: bfloat16 [1024, 1024], P('tensor', 'dp'), may hold values from -0.1875 to 0.1875
- channel_key_weight: bfloat16 [1024, 4096], P('dp', 'tensor'), may hold values from -0.1875 to 0.1875
- channel_value_weight: bfloat16 [4096, 1024], P('tensor', 'dp'), may hold values from -0.09375 to 0.09375
Outputs:
- block_out: bfloat16 [8192, 1024], P(('dp', 'tensor'))
- loss: float32 [], replicated
- grad_in: float32 [8192, 1024], P(('dp', 'tensor'))
- grad_v_first: float32 [8192, 1024], P('dp', 'tensor')
- grad_norm_gain: float32 [2, 1024], replicated
- grad_norm_bias: float32 [2, 1024], replicated
- grad_lerps: float32 [6, 1024], replicated
- grad_decay_lerp: float32 [1024], replicated
- grad_decay_base: float32 [1024], replicated
- grad_head_gain: float32 [3, 1024], replicated
- grad_head_bias: float32 [4, 1024], replicated
- grad_lora_down: float32 [1024, 288], replicated
- grad_lora_up: float32 [288, 1024], replicated
- grad_rkv: float32 [3, 1024, 1024], P(None, 'dp', 'tensor')
- grad_out_weight: float32 [1024, 1024], P('tensor', 'dp')
- grad_key_weight: float32 [1024, 4096], P('dp', 'tensor')
- grad_value_weight: float32 [4096, 1024], P('tensor', 'dp')
Inputs may be any that keep to these rules, and one draw needn't show every extreme that they name: `segments`: segment numbers start at 0 and rise by one from document to document along a sequence; every sequence holds max(2, 2) documents, each of at least min(60, 512 // (2 * max(2, 2))) and at most min(800, 384) tokens, and one of exactly that most.
All inputs are finite; a program needn't handle non-finite values.
Results may differ from a plain program's by a relative error of at most 0.017.
Values may be sent and summed in bfloat16 or wider, within the bound.
No kernel may reach another device: no remote copies, remote signals or barrier semaphores. Data moves between devices by JAX's collectives and lax.ppermute only.
A program may use at most 448 MiB of HBM per device.

v0:
```python
import jax
import jax.numpy as jnp
from jax import lax
from jax.experimental import pallas as pl
from jax.experimental.pallas import tpu as pltpu
from jax.sharding import PartitionSpec as P

HEAD_SIZE = 64
CHUNK = 64
PAIR = 2 * HEAD_SIZE
BF = jnp.bfloat16
F32 = jnp.float32
DECAY_SCALE = 0.6065306597126334
DECAY_MAP_RANK = 64
RATE_MAP_RANK = 64
VALUE_MIX_RANK = 32


def matrix_multiply(left, right):
    return jnp.dot(left, right, preferred_element_type=jnp.float32)


def matmul_tn(left, right):
    return lax.dot_general(
        left, right, (((0,), (0,)), ((), ())), preferred_element_type=jnp.float32
    )


def matrix_multiply_transposed(left, right):
    return lax.dot_general(
        left, right, (((1,), (1,)), ((), ())), preferred_element_type=jnp.float32
    )


def layer_norm(row_data, gain_row, bias_row):
    row_mean = jnp.mean(row_data, -1, keepdims=True)
    centred = row_data - row_mean
    variance = jnp.mean(centred * centred, -1, keepdims=True)
    return centred * lax.rsqrt(variance + 1e-05) * gain_row + bias_row


def shift_down(row_data, retain_mask):
    return jnp.concatenate([jnp.zeros_like(row_data[:1]), row_data[:-1]], 0) * retain_mask[:, None]


def shift_up(row_data, retain_mask):
    moved = row_data * retain_mask[:, None]
    return jnp.concatenate([moved[1:], jnp.zeros_like(moved[:1])], 0)


def add_rows(full_rows, extra_rows, first_row):
    current = lax.dynamic_slice_in_dim(full_rows, first_row, extra_rows.shape[0], 0)
    return lax.dynamic_update_slice_in_dim(full_rows, current + extra_rows, first_row, 0)


def place_cols(col_block, total_cols, first_col):
    zeros_full = jnp.zeros(col_block.shape[:-1] + (total_cols,), jnp.float32)
    return lax.dynamic_update_slice_in_dim(zeros_full, col_block, first_col, col_block.ndim - 1)


NN = (((1,), (0,)), ((), ()))
NT = (((1,), (1,)), ((), ()))
TN = (((0,), (0,)), ((), ()))


def split(x, terms=2):
    hi = x.astype(BF)
    if terms == 1:
        return (hi,)
    return (hi, (x - hi.astype(F32)).astype(BF))


def mm(a, b, dims):
    out = lax.dot_general(a[0], b[0], dims, preferred_element_type=F32)
    if len(b) > 1:
        out = out + lax.dot_general(a[0], b[1], dims, preferred_element_type=F32)
    if len(a) > 1:
        out = out + lax.dot_general(a[1], b[0], dims, preferred_element_type=F32)
    return out


def rows_of(*parts):
    return tuple(jnp.concatenate(terms, 0) for terms in zip(*parts))


def cols_of(*parts):
    return tuple(jnp.concatenate(terms, 1) for terms in zip(*parts))


def spread(parts, left, right):
    return tuple(jnp.concatenate([x * left, x * right], 0) for x in parts)


def chunk_masks(gcol, aux):
    size = 2 * CHUNK
    row = lax.broadcasted_iota(jnp.int32, (size, size), 0)
    lane = lax.broadcasted_iota(jnp.int32, (size, size), 1)
    t_row, t_lane = row & (CHUNK - 1), lane & (CHUNK - 1)
    same_head = (row >= CHUNK) == (lane >= CHUNK)
    g_row = jnp.concatenate([gcol, gcol], 0)
    linked = (g_row == aux[0:1, :]) & same_head
    strict = linked & (t_row > t_lane)
    upto = linked & (t_row >= t_lane)
    from_start = (gcol == aux[2:3, :]).astype(F32)
    to_end = (gcol == aux[1:2, :]).astype(F32)
    end_clear = (aux[1:2, :] == aux[2:3, :]).astype(F32)
    return row, lane, t_row, t_lane, strict, upto, from_start, to_end, end_clear


def head_sum(x, ones):
    return mm(split(x), (ones,), NN)


def lane_masks():
    lane = lax.broadcasted_iota(jnp.int32, (1, PAIR), 1)
    left = (lane < HEAD_SIZE).astype(F32)
    return left.astype(BF), (1.0 - left).astype(BF), left


def head_ones():
    row = lax.broadcasted_iota(jnp.int32, (PAIR, PAIR), 0)
    lane = lax.broadcasted_iota(jnp.int32, (PAIR, PAIR), 1)
    return ((row >= HEAD_SIZE) == (lane >= HEAD_SIZE)).astype(F32).astype(BF)


def lower_ones():
    row = lax.broadcasted_iota(jnp.int32, (CHUNK, CHUNK), 0)
    lane = lax.broadcasted_iota(jnp.int32, (CHUNK, CHUNK), 1)
    return (row >= lane).astype(F32).astype(BF)


def split3(x):
    hi = x.astype(BF)
    rest = x - hi.astype(F32)
    mid = rest.astype(BF)
    return (hi, mid, (rest - mid.astype(F32)).astype(BF))


def ones_times(ones, x, dims):
    total = None
    for term in split3(x):
        part = lax.dot_general(ones, term, dims, preferred_element_type=F32)
        total = part if total is None else total + part
    return total


def sigmoid(x):
    return jax.nn.sigmoid(x)


def pair_values(refs, par, cols, ones):
    r_ref, kp_ref, vp_ref, ew_ref, ea_ref, ev_ref, vf_ref = refs
    out = {}
    r, kp, vp = r_ref[:, cols], kp_ref[:, cols], vp_ref[:, cols]
    vf = vf_ref[:, cols].astype(F32)
    a = sigmoid(par[4:5] + ea_ref[:, cols])
    s = sigmoid(par[5:6] + ev_ref[:, cols])
    v = vp + (vf - vp) * s
    sg = sigmoid(par[0:1] + ew_ref[:, cols])
    ld = -DECAY_SCALE * sg
    u = kp * par[1:2]
    inv = lax.rsqrt(head_sum(u * u, ones) + 1e-06)
    kk = u * inv
    k = kp * (1.0 + (a - 1.0) * par[2:3])
    out.update(r=r, kp=kp, vp=vp, vf=vf, a=a, s=s, v=v, sg=sg, ld=ld, inv=inv, kk=kk, k=k)
    return out


def chunk_values(w, lower, from_start, to_end, end_clear):
    inc = ones_times(lower, w["ld"], NN)
    exc = inc - w["ld"]
    last = inc[CHUNK - 1 : CHUNK, :]
    w["e_inc"] = jnp.exp(inc)
    w["e_exc"] = jnp.exp(exc)
    w["e_neg"] = jnp.exp(-inc)
    w["carry"] = jnp.exp(last - inc) * to_end
    w["finish"] = jnp.exp(last) * end_clear
    w["b"] = w["kk"] * w["a"]
    w["kappa"] = w["kk"] * w["e_exc"]
    w["rho"] = w["r"] * w["e_inc"]
    w["key_hat"] = w["k"] * w["e_neg"]
    w["take_hat"] = w["b"] * w["e_neg"]
    w["k_end"] = w["k"] * w["carry"]
    w["b_end"] = w["b"] * w["carry"]
    w["kappa0"] = w["kappa"] * from_start
    w["rho0"] = w["rho"] * from_start


def forward_kernel(
    r_ref, kp_ref, vp_ref, ew_ref, ea_ref, ev_ref, gate_ref, vf_ref, par_ref, gcol_ref, aux_ref,
    z_ref, y_ref, q_ref, t_ref, akk_ref, ark_ref, arb_ref, s0_ref, state,
):
    pairs = r_ref.shape[1] // PAIR

    @pl.when(pl.program_id(0) == 0)
    def _():
        state[...] = jnp.zeros_like(state)

    masks = chunk_masks(gcol_ref[...], aux_ref[0])
    row, lane, t_row, t_lane, strict, upto, from_start, to_end, end_clear = masks
    left, right, left_f = lane_masks()
    ones = head_ones()
    lower = lower_ones()
    eye = (row == lane).astype(F32)
    in8 = (t_row >> 3) == (t_lane >> 3)
    levels = []
    for bits in (3, 4, 5):
        levels.append(((t_row >> (bits + 1)) == (t_lane >> (bits + 1))) & ((t_row >> bits) != (t_lane >> bits)))
    group = range(pairs)
    cols = [slice(p * PAIR, (p + 1) * PAIR) for p in group]
    refs = (r_ref, kp_ref, vp_ref, ew_ref, ea_ref, ev_ref, vf_ref)
    pars = [par_ref[:, cols[p]] for p in group]
    w = [pair_values(refs, pars[p], cols[p], ones) for p in group]
    for p in group:
        chunk_values(w[p], lower, from_start, to_end, end_clear)
    akk, akb, ark, arb = [], [], [], []
    for p in group:
        x = w[p]
        rows = rows_of(spread(split(x["kappa"]), left, right), spread(split(x["rho"]), left, right))
        keys = rows_of(spread(split(x["key_hat"]), left, right), spread(split(x["take_hat"]), left, right))
        scores = mm(rows, keys, NT)
        n = 2 * CHUNK
        akk.append(jnp.where(strict, scores[:n, :n], 0.0))
        akb.append(jnp.where(strict, scores[:n, n:], 0.0))
        ark.append(jnp.where(upto, scores[n:, :n], 0.0))
        arb.append(jnp.where(upto, scores[n:, n:], 0.0))
    neg = [jnp.where(in8, -akb[p], 0.0) for p in group]
    neg_s = [split(x) for x in neg]
    two = [mm(x, x, NN) for x in neg_s]
    two_s = [split(x) for x in two]
    both = [mm(rows_of(neg_s[p], two_s[p]), two_s[p], NN) for p in group]
    n = 2 * CHUNK
    low = [neg[p] + two[p] + both[p][:n] for p in group]
    four = [both[p][n:] for p in group]
    inv = [eye + low[p] + four[p] + mm(split(low[p]), split(four[p]), NN) for p in group]
    for level in levels:
        inv_s = [split(x) for x in inv]
        mid = [mm(split(jnp.where(level, akb[p], 0.0)), inv_s[p], NN) for p in group]
        inv = [inv[p] - mm(inv_s[p], split(mid[p]), NN) for p in group]
    inv_s = [split(x) for x in inv]
    v_s = [spread(split(w[p]["v"]), left, right) for p in group]
    akk_v = [mm(split(akk[p]), v_s[p], NN) for p in group]
    s0 = [state[p] for p in group]
    carried = [
        mm(
            rows_of(spread(split(w[p]["kappa0"]), left, right), spread(split(w[p]["rho0"]), left, right)),
            split(s0[p]),
            NT,
        )
        for p in group
    ]
    q = [mm(inv_s[p], split(carried[p][:n] + akk_v[p]), NN) for p in group]
    q_s = [split(x) for x in q]
    y2 = [
        carried[p][n:] + mm(cols_of(split(ark[p]), split(-arb[p])), rows_of(v_s[p], q_s[p]), NN)
        for p in group
    ]
    for p in group:
        x = w[p]
        ends = rows_of(spread(split(x["k_end"]), left, right), spread(split(-x["b_end"]), left, right))
        state[p] = s0[p] * x["finish"] + mm(rows_of(v_s[p], q_s[p]), ends, TN)
        y = y2[p][:CHUNK] + y2[p][CHUNK:]
        y_ref[:, cols[p]] = y
        q_ref[:, cols[p]] = q[p][:CHUNK] + q[p][CHUNK:]
        t_ref[0, p] = inv[p]
        akk_ref[0, p] = akk[p]
        ark_ref[0, p] = ark[p]
        arb_ref[0, p] = arb[p]
        s0_ref[0, p] = s0[p]
        par = pars[p]
        centred = y - head_sum(y, ones) * (1.0 / HEAD_SIZE)
        var = head_sum(centred * centred, ones) * (1.0 / HEAD_SIZE)
        normed = centred * lax.rsqrt(var + HEAD_SIZE * 0.01)
        bonus = head_sum(x["r"] * x["k"] * par[6:7], ones)
        z = (normed * par[3:4] + par[7:8] + bonus * x["v"]) * gate_ref[:, cols[p]]
        z_ref[:, cols[p]] = z.astype(z_ref.dtype)


def backward_kernel(
    dz_ref, r_ref, kp_ref, vp_ref, ew_ref, ea_ref, ev_ref, gate_ref, vf_ref, par_ref, gcol_ref, aux_ref,
    y_ref, q_ref, t_ref, akk_ref, ark_ref, arb_ref, s0_ref,
    dr_ref, dkp_ref, dvp_ref, dew_ref, dea_ref, dev_ref, dgate_ref, dvf_ref, dpar_ref, state,
):
    pairs = r_ref.shape[1] // PAIR
    n = 2 * CHUNK

    @pl.when(pl.program_id(0) == 0)
    def _():
        state[...] = jnp.zeros_like(state)
        dpar_ref[...] = jnp.zeros_like(dpar_ref)

    masks = chunk_masks(gcol_ref[...], aux_ref[0])
    row, lane, t_row, t_lane, strict, upto, from_start, to_end, end_clear = masks
    left, right, left_f = lane_masks()
    ones = head_ones()
    lower = lower_ones()
    last_row = (lax.broadcasted_iota(jnp.int32, (CHUNK, 1), 0) == CHUNK - 1).astype(F32)
    group = range(pairs)
    cols = [slice(p * PAIR, (p + 1) * PAIR) for p in group]
    refs = (r_ref, kp_ref, vp_ref, ew_ref, ea_ref, ev_ref, vf_ref)
    pars = [par_ref[:, cols[p]] for p in group]
    w = [pair_values(refs, pars[p], cols[p], ones) for p in group]
    scale = 1.0 / HEAD_SIZE
    for p in group:
        x, par = w[p], pars[p]
        chunk_values(x, lower, from_start, to_end, end_clear)
        y = y_ref[:, cols[p]]
        centred = y - head_sum(y, ones) * scale
        var = head_sum(centred * centred, ones) * scale
        istd = lax.rsqrt(var + HEAD_SIZE * 0.01)
        normed = centred * istd
        rk = x["r"] * x["k"]
        bonus = head_sum(rk * par[6:7], ones)
        dz = dz_ref[:, cols[p]]
        dgate_ref[:, cols[p]] = (dz * (normed * par[3:4] + par[7:8] + bonus * x["v"])).astype(BF)
        do = dz * gate_ref[:, cols[p]]
        dbonus = head_sum(do * x["v"], ones)
        x["dv"] = do * bonus
        x["dr"] = dbonus * x["k"] * par[6:7]
        x["dk"] = dbonus * x["r"] * par[6:7]
        dn = do * par[3:4]
        x["dy"] = istd * (dn - head_sum(dn, ones) * scale - normed * (head_sum(dn * normed, ones) * scale))
        x["g2"] = jnp.sum(do * normed, 0, keepdims=True)
        x["b3"] = jnp.sum(do, 0, keepdims=True)
        x["b2"] = jnp.sum(dbonus * rk, 0, keepdims=True)
    dy_s = [spread(split(w[p]["dy"]), left, right) for p in group]
    v_s = [spread(split(w[p]["v"]), left, right) for p in group]
    q_s = [spread(split(q_ref[:, cols[p]]), left, right) for p in group]
    ds = [state[p] for p in group]
    ds_s = [split(ds[p]) for p in group]
    kend_s = [spread(split(w[p]["k_end"]), left, right) for p in group]
    bend_s = [spread(split(w[p]["b_end"]), left, right) for p in group]
    from_end = [mm(rows_of(kend_s[p], bend_s[p]), ds_s[p], NT) for p in group]
    dq = [-(mm(split(arb_ref[0, p]), dy_s[p], TN) + from_end[p][n:]) for p in group]
    du = [mm(split(t_ref[0, p]), split(dq[p]), TN) for p in group]
    du_s = [split(du[p]) for p in group]
    uy_s = [rows_of(du_s[p], dy_s[p]) for p in group]
    s0 = [s0_ref[0, p] for p in group]
    kappa_s = [spread(split(w[p]["kappa"]), left, right) for p in group]
    rho_s = [spread(split(w[p]["rho"]), left, right) for p in group]
    for p in group:
        x = w[p]
        start = rows_of(spread(split(x["kappa0"]), left, right), spread(split(x["rho0"]), left, right))
        state[p] = ds[p] * x["finish"] + mm(uy_s[p], start, TN)
    dv2 = [
        from_end[p][:n] + mm(rows_of(split(akk_ref[0, p]), split(ark_ref[0, p])), uy_s[p], TN)
        for p in group
    ]
    start_grad = [mm(uy_s[p], split(s0[p]), NN) for p in group]
    end_grad = [mm(rows_of(v_s[p], q_s[p]), ds_s[p], NN) for p in group]
    vq_s = [rows_of(v_s[p], tuple(-t for t in q_s[p])) for p in group]
    raw = [mm(uy_s[p], vq_s[p], NT) for p in group]
    da_s = []
    for p in group:
        top = jnp.where(jnp.concatenate([strict, strict], 1), raw[p][:n], 0.0)
        bottom = jnp.where(jnp.concatenate([upto, upto], 1), raw[p][n:], 0.0)
        da_s.append(split(jnp.concatenate([top, bottom], 0)))
    row_grad = [
        mm(
            da_s[p],
            rows_of(spread(split(w[p]["key_hat"]), left, right), spread(split(w[p]["take_hat"]), left, right)),
            NN,
        )
        for p in group
    ]
    col_grad = [mm(da_s[p], rows_of(kappa_s[p], rho_s[p]), TN) for p in group]

    def fold(z):
        return z[:CHUNK] + z[CHUNK:n], z[n : n + CHUNK] + z[n + CHUNK :]

    for p in group:
        x, par = w[p], pars[p]
        dkappa0, drho0 = fold(start_grad[p])
        dkend, dbend = fold(end_grad[p])
        dbend = -dbend
        dkappa, drho = fold(row_grad[p])
        dkey, dtake = fold(col_grad[p])
        dkappa = dkappa + dkappa0 * from_start
        drho = drho + drho0 * from_start
        dv = x["dv"] + dv2[p][:CHUNK] + dv2[p][CHUNK:]
        dr = x["dr"] + drho * x["e_inc"]
        dk = x["dk"] + dkey * x["e_neg"] + dkend * x["carry"]
        db = dtake * x["e_neg"] + dbend * x["carry"]
        dkk = dkappa * x["e_exc"] + db * x["a"]
        da = db * x["kk"]
        dexc = dkappa * x["kappa"]
        dends = dkend * x["k_end"] + dbend * x["b_end"]
        dinc = drho * x["rho"] - dkey * x["key_hat"] - dtake * x["take_hat"] - dends
        dlast = jnp.sum(dends, 0, keepdims=True) + jnp.sum(s0[p] * ds[p], 0, keepdims=True) * x["finish"]
        dld = ones_times(lower, dinc + dexc + last_row * dlast, TN) - dexc
        dkp = dk * (1.0 + (x["a"] - 1.0) * par[2:3])
        da = da + dk * x["kp"] * par[2:3]
        g1 = jnp.sum(dk * x["kp"] * (x["a"] - 1.0), 0, keepdims=True)
        dunit = x["inv"] * (dkk - x["kk"] * head_sum(dkk * x["kk"], ones))
        dkp = dkp + dunit * par[1:2]
        g0 = jnp.sum(dunit * x["kp"], 0, keepdims=True)
        dev = dv * (x["vf"] - x["vp"]) * x["s"] * (1.0 - x["s"])
        dea = da * x["a"] * (1.0 - x["a"])
        dew = dld * (-DECAY_SCALE) * x["sg"] * (1.0 - x["sg"])
        dr_ref[:, cols[p]] = dr.astype(BF)
        dkp_ref[:, cols[p]] = dkp.astype(BF)
        dvp_ref[:, cols[p]] = (dv * (1.0 - x["s"])).astype(BF)
        dvf_ref[:, cols[p]] = dv * x["s"]
        dew_ref[:, cols[p]] = dew.astype(BF)
        dea_ref[:, cols[p]] = dea.astype(BF)
        dev_ref[:, cols[p]] = dev.astype(BF)
        dpar_ref[:, cols[p]] += jnp.concatenate(
            [
                jnp.sum(dew, 0, keepdims=True),
                g0,
                g1,
                x["g2"],
                jnp.sum(dea, 0, keepdims=True),
                jnp.sum(dev, 0, keepdims=True),
                x["b2"],
                x["b3"],
            ],
            0,
        )


def token_spec(cols, order):
    return pl.BlockSpec((CHUNK, cols), lambda i: (order(i), 0))


def square_spec(pairs, order):
    return pl.BlockSpec((1, pairs, PAIR, PAIR), lambda i: (order(i), 0, 0, 0))


def mixer_forward(r, kp, vp, ew, ea, ev, gate, vf, par, gcol, aux):
    tokens, cols = r.shape
    steps, pairs = tokens // CHUNK, cols // PAIR
    order = lambda i: i
    tok = token_spec(cols, order)
    sq = square_spec(pairs, order)
    sq_shape = jax.ShapeDtypeStruct((steps, pairs, PAIR, PAIR), F32)
    tok_shape = jax.ShapeDtypeStruct((tokens, cols), F32)
    flops = steps * pairs * 19 * 3 * 2 * PAIR**3
    return pl.pallas_call(
        forward_kernel,
        name="mixer_forward",
        grid=(steps,),
        in_specs=[tok] * 8
        + [
            pl.BlockSpec((8, cols), lambda i: (0, 0)),
            pl.BlockSpec((CHUNK, 1), lambda i: (i, 0)),
            pl.BlockSpec((1, 8, PAIR), lambda i: (i, 0, 0)),
        ],
        out_specs=[tok, tok, tok] + [sq] * 5,
        out_shape=[jax.ShapeDtypeStruct((tokens, cols), BF), tok_shape, tok_shape] + [sq_shape] * 5,
        scratch_shapes=[pltpu.VMEM((pairs, PAIR, PAIR), F32)],
        compiler_params=pltpu.CompilerParams(vmem_limit_bytes=48 << 20),
        cost_estimate=pl.CostEstimate(flops=flops, bytes_accessed=22 << 20, transcendentals=8 * tokens * cols),
    )(r, kp, vp, ew, ea, ev, gate, vf, par, gcol, aux)


def mixer_backward(dz, r, kp, vp, ew, ea, ev, gate, vf, par, gcol, aux, y, q, t, akk, ark, arb, s0):
    tokens, cols = r.shape
    steps, pairs = tokens // CHUNK, cols // PAIR
    order = lambda i: steps - 1 - i
    tok = token_spec(cols, order)
    sq = square_spec(pairs, order)
    low = jax.ShapeDtypeStruct((tokens, cols), BF)
    flops = steps * pairs * 15 * 3 * 2 * PAIR**3
    return pl.pallas_call(
        backward_kernel,
        name="mixer_backward",
        grid=(steps,),
        in_specs=[tok] * 9
        + [
            pl.BlockSpec((8, cols), lambda i: (0, 0)),
            pl.BlockSpec((CHUNK, 1), lambda i: (order(i), 0)),
            pl.BlockSpec((1, 8, PAIR), lambda i: (order(i), 0, 0)),
        ]
        + [tok, tok]
        + [sq] * 5,
        out_specs=[tok] * 8 + [pl.BlockSpec((8, cols), lambda i: (0, 0))],
        out_shape=[low] * 7
        + [jax.ShapeDtypeStruct((tokens, cols), F32), jax.ShapeDtypeStruct((8, cols), F32)],
        scratch_shapes=[pltpu.VMEM((pairs, PAIR, PAIR), F32)],
        compiler_params=pltpu.CompilerParams(vmem_limit_bytes=48 << 20),
        cost_estimate=pl.CostEstimate(flops=flops, bytes_accessed=28 << 20, transcendentals=8 * tokens * cols),
    )(dz, r, kp, vp, ew, ea, ev, gate, vf, par, gcol, aux, y, q, t, akk, ark, arb, s0)


def document_tables(segments):
    rows, length = segments.shape
    marks = segments + (length + 1) * lax.broadcasted_iota(jnp.int32, (rows, length), 0)
    flat = marks.reshape(-1).astype(F32)
    blocks = flat.reshape(-1, CHUNK)
    ends = blocks[:, -1]
    before = jnp.concatenate([jnp.full((1,), -1.0, F32), ends[:-1]])
    wide = lambda x: jnp.broadcast_to(x[:, None], (x.shape[0], PAIR))
    aux = jnp.stack([jnp.concatenate([blocks, blocks], 1), wide(ends), wide(before)] + [jnp.zeros((blocks.shape[0], PAIR), F32)] * 5, 1)
    return flat[:, None], aux


def on_device(
    block_input,
    first_layer_values,
    segments,
    valid,
    cotangent,
    teacher,
    layer_norm_gain,
    layer_norm_bias,
    lerps,
    decay_offset,
    head_gain_table,
    per_unit_shift_array,
    lowrank_first_maps,
    lowrank_second_maps,
    receptance_key_value_weight,
    time_output_weight,
    channel_key_weight,
    channel_value_weight,
):
    tensor_size = lax.axis_size("tensor")
    tensor_pos = lax.axis_index("tensor")
    dp_pos = lax.axis_index("dp")
    own_rows = block_input.shape[0]
    model_width = block_input.shape[1]
    local_columns = receptance_key_value_weight.shape[2]
    column_begin = tensor_pos * local_columns
    row_begin = tensor_pos * own_rows
    divide_pair = DECAY_MAP_RANK + RATE_MAP_RANK
    divide_three = divide_pair + VALUE_MIX_RANK
    valid_rows = valid.astype(jnp.float32).reshape(-1)
    valid_token_count = jnp.sum(valid_rows)
    valid_own = lax.dynamic_slice_in_dim(
        valid_rows, (dp_pos * tensor_size + tensor_pos) * own_rows, own_rows
    )
    same_doc = (segments[:, 1:] == segments[:, :-1]).astype(jnp.float32)
    retain_mask = jnp.concatenate(
        [jnp.zeros((segments.shape[0], 1), jnp.float32), same_doc], 1
    ).reshape(-1)
    rkv_full, out_full, key_full, value_full = (
        lax.all_gather(receptance_key_value_weight, "dp", axis=1, tiled=True),
        lax.all_gather(time_output_weight, "dp", axis=1, tiled=True),
        lax.all_gather(channel_key_weight, "dp", axis=0, tiled=True),
        lax.all_gather(channel_value_weight, "dp", axis=1, tiled=True),
    )
    block_row_slice = block_input.astype(jnp.float32)
    normed_one, norm_one_back = jax.vjp(
        layer_norm, block_row_slice, layer_norm_gain[0], layer_norm_bias[0]
    )
    gathered = lax.all_gather(normed_one.astype(jnp.bfloat16), "tensor", axis=0, tiled=True).astype(
        jnp.float32
    )
    delta_one = shift_down(gathered, retain_mask) - gathered
    blended = [
        (gathered + delta_one * lerps[lane_index]).astype(jnp.bfloat16) for lane_index in range(6)
    ]
    acceptance_vector_lines = matrix_multiply(blended[0], rkv_full[0])
    key_projected = matrix_multiply(blended[2], rkv_full[1])
    value_projected = matrix_multiply(blended[3], rkv_full[2])
    decay_squashed = jnp.tanh(matrix_multiply(blended[1], lowrank_first_maps[:, :DECAY_MAP_RANK]))
    decay_inner = decay_squashed.astype(jnp.bfloat16)
    rate_inner = matrix_multiply(
        blended[4], lowrank_first_maps[:, DECAY_MAP_RANK:divide_pair]
    ).astype(jnp.bfloat16)
    value_inner = matrix_multiply(
        blended[3], lowrank_first_maps[:, divide_pair:divide_three]
    ).astype(jnp.bfloat16)
    gate_squashed = jax.nn.sigmoid(
        matrix_multiply(blended[5], lowrank_first_maps[:, divide_three:])
    )
    gate_inner = gate_squashed.astype(jnp.bfloat16)
    upper_columns = lax.dynamic_slice_in_dim(lowrank_second_maps, column_begin, local_columns, 1)
    decay_lowrank = matrix_multiply(decay_inner, upper_columns[:DECAY_MAP_RANK])
    rate_lowrank = matrix_multiply(rate_inner, upper_columns[DECAY_MAP_RANK:divide_pair])
    value_lowrank = matrix_multiply(value_inner, upper_columns[divide_pair:divide_three])
    output_switch_thin_factors = matrix_multiply(gate_inner, upper_columns[divide_three:])
    base_cols = lax.dynamic_slice_in_dim(decay_offset, column_begin, local_columns, 0)
    gain_cols = lax.dynamic_slice_in_dim(head_gain_table, column_begin, local_columns, 1)
    bias_cols = lax.dynamic_slice_in_dim(per_unit_shift_array, column_begin, local_columns, 1)
    par = jnp.concatenate([base_cols[None], gain_cols, bias_cols], 0)
    doc_col, doc_aux = document_tables(segments)
    mixer_low, *kept = mixer_forward(
        acceptance_vector_lines,
        key_projected,
        value_projected,
        decay_lowrank,
        rate_lowrank,
        value_lowrank,
        output_switch_thin_factors,
        first_layer_values,
        par,
        doc_col,
        doc_aux,
    )
    attended = lax.psum_scatter(
        matrix_multiply(mixer_low, out_full), "tensor", scatter_dimension=0, tiled=True
    )
    after_mixer = block_row_slice + attended
    normed_two, norm_two_back = jax.vjp(
        layer_norm, after_mixer, layer_norm_gain[1], layer_norm_bias[1]
    )
    gathered_two = lax.all_gather(
        normed_two.astype(jnp.bfloat16), "tensor", axis=0, tiled=True
    ).astype(jnp.float32)
    delta_two = shift_down(gathered_two, retain_mask) - gathered_two
    channel_in = (gathered_two + delta_two * lerps[6]).astype(jnp.bfloat16)
    channel_pre = matrix_multiply(channel_in, key_full)
    rectified = jnp.maximum(channel_pre, 0.0)
    hidden_low = (rectified * rectified).astype(jnp.bfloat16)
    channel = lax.psum_scatter(
        matrix_multiply(hidden_low, value_full), "tensor", scatter_dimension=0, tiled=True
    )
    block_sum = after_mixer + channel
    mismatch = block_sum - teacher.astype(jnp.float32)
    loss_part = jnp.sum(valid_own[:, None] * mismatch * mismatch) / (
        valid_token_count * model_width
    )
    seed = valid_own[:, None] * (
        cotangent.astype(jnp.float32) + 2.0 * mismatch / (valid_token_count * model_width)
    )
    seed_all = lax.all_gather(seed.astype(jnp.bfloat16), "tensor", axis=0, tiled=True)
    grad_value_part = matmul_tn(hidden_low, seed_all)
    hidden_grad = matrix_multiply_transposed(seed_all, value_full)
    pre_grad = (hidden_grad * 2.0 * rectified).astype(jnp.bfloat16)
    grad_key_part = matmul_tn(channel_in, pre_grad)
    channel_grad = matrix_multiply_transposed(pre_grad, key_full)
    lerp_six = jnp.sum(channel_grad * delta_two, 0)
    spread_two = channel_grad * (1.0 - lerps[6]) + shift_up(channel_grad * lerps[6], retain_mask)
    normed_two_grad = lax.psum_scatter(spread_two, "tensor", scatter_dimension=0, tiled=True)
    mixer_sum_grad, gain_two, bias_two = norm_two_back(normed_two_grad)
    after_grad = seed + mixer_sum_grad
    attended_all = lax.all_gather(after_grad.astype(jnp.bfloat16), "tensor", axis=0, tiled=True)
    grad_out_part = matmul_tn(mixer_low, attended_all)
    mixer_grad = matrix_multiply_transposed(attended_all, out_full)
    (
        recept_low,
        key_low,
        value_low,
        decay_low,
        rate_low,
        vlora_low,
        gate_low,
        first_grad,
        par_grad,
    ) = mixer_backward(
        mixer_grad,
        acceptance_vector_lines,
        key_projected,
        value_projected,
        decay_lowrank,
        rate_lowrank,
        value_lowrank,
        output_switch_thin_factors,
        first_layer_values,
        par,
        doc_col,
        doc_aux,
        *kept,
    )
    base_grad, gain_grad, bias_grad = par_grad[0], par_grad[1:4], par_grad[4:8]
    grad_rkv_part = jnp.stack(
        [
            matmul_tn(blended[0], recept_low),
            matmul_tn(blended[2], key_low),
            matmul_tn(blended[3], value_low),
        ]
    )
    grad_up_cols = jnp.concatenate(
        [
            matmul_tn(decay_inner, decay_low),
            matmul_tn(rate_inner, rate_low),
            matmul_tn(value_inner, vlora_low),
            matmul_tn(gate_inner, gate_low),
        ],
        0,
    )
    hidden_grads = jnp.concatenate(
        [
            matrix_multiply_transposed(decay_low, upper_columns[:DECAY_MAP_RANK])
            * (1.0 - decay_squashed * decay_squashed),
            matrix_multiply_transposed(rate_low, upper_columns[DECAY_MAP_RANK:divide_pair]),
            matrix_multiply_transposed(vlora_low, upper_columns[divide_pair:divide_three]),
            matrix_multiply_transposed(gate_low, upper_columns[divide_three:])
            * gate_squashed
            * (1.0 - gate_squashed),
        ],
        1,
    )
    hidden_local = lax.psum_scatter(hidden_grads, "tensor", scatter_dimension=0, tiled=True).astype(
        jnp.bfloat16
    )
    own_mixed = [
        lax.dynamic_slice_in_dim(blended[lane_index], row_begin, own_rows, 0)
        for lane_index in (1, 4, 3, 5)
    ]
    grad_down = jnp.concatenate(
        [
            matmul_tn(own_mixed[0], hidden_local[:, :DECAY_MAP_RANK]),
            matmul_tn(own_mixed[1], hidden_local[:, DECAY_MAP_RANK:divide_pair]),
            matmul_tn(own_mixed[2], hidden_local[:, divide_pair:divide_three]),
            matmul_tn(own_mixed[3], hidden_local[:, divide_three:]),
        ],
        1,
    )
    blank_rows = jnp.zeros(gathered.shape, jnp.float32)
    mixed_grads = [
        matrix_multiply_transposed(recept_low, rkv_full[0]),
        add_rows(
            blank_rows,
            matrix_multiply_transposed(
                hidden_local[:, :DECAY_MAP_RANK], lowrank_first_maps[:, :DECAY_MAP_RANK]
            ),
            row_begin,
        ),
        matrix_multiply_transposed(key_low, rkv_full[1]),
        add_rows(
            matrix_multiply_transposed(value_low, rkv_full[2]),
            matrix_multiply_transposed(
                hidden_local[:, divide_pair:divide_three],
                lowrank_first_maps[:, divide_pair:divide_three],
            ),
            row_begin,
        ),
        add_rows(
            blank_rows,
            matrix_multiply_transposed(
                hidden_local[:, DECAY_MAP_RANK:divide_pair],
                lowrank_first_maps[:, DECAY_MAP_RANK:divide_pair],
            ),
            row_begin,
        ),
        add_rows(
            blank_rows,
            matrix_multiply_transposed(
                hidden_local[:, divide_three:], lowrank_first_maps[:, divide_three:]
            ),
            row_begin,
        ),
    ]
    spread_one = blank_rows
    carried = blank_rows
    lerp_rows = []
    for lane_index in range(6):
        lane_grad = mixed_grads[lane_index]
        lerp_rows.append(jnp.sum(lane_grad * delta_one, 0))
        spread_one = spread_one + lane_grad * (1.0 - lerps[lane_index])
        carried = carried + lane_grad * lerps[lane_index]
    spread_one = spread_one + shift_up(carried, retain_mask)
    normed_one_grad = lax.psum_scatter(spread_one, "tensor", scatter_dimension=0, tiled=True)
    input_grad, gain_one, bias_one = norm_one_back(normed_one_grad)
    grad_in = after_grad + input_grad
    small_terms = (
        jnp.stack([gain_one, gain_two]),
        jnp.stack([bias_one, bias_two]),
        jnp.stack(lerp_rows + [lerp_six]),
        place_cols(base_grad, model_width, column_begin),
        place_cols(gain_grad, model_width, column_begin),
        place_cols(bias_grad, model_width, column_begin),
        grad_down,
        place_cols(grad_up_cols, model_width, column_begin),
        loss_part,
    )
    summed = lax.psum(
        (
            small_terms[0],
            small_terms[1],
            small_terms[2],
            small_terms[3],
            small_terms[4],
            small_terms[5],
            small_terms[6],
            small_terms[7],
            small_terms[8],
        ),
        ("dp", "tensor"),
    )
    grad_rkv, grad_out_weight, grad_key_weight, grad_value_weight = (
        lax.psum_scatter(grad_rkv_part, "dp", scatter_dimension=1, tiled=True),
        lax.psum_scatter(grad_out_part, "dp", scatter_dimension=1, tiled=True),
        lax.psum_scatter(grad_key_part, "dp", scatter_dimension=0, tiled=True),
        lax.psum_scatter(grad_value_part, "dp", scatter_dimension=1, tiled=True),
    )
    lerp_summed = summed[2]
    return (
        block_sum.astype(jnp.bfloat16),
        summed[8],
        grad_in,
        first_grad,
        summed[0],
        summed[1],
        jnp.concatenate([lerp_summed[:1], lerp_summed[2:]], 0),
        lerp_summed[1],
        summed[3],
        summed[4],
        summed[5],
        summed[6],
        summed[7],
        grad_rkv,
        grad_out_weight,
        grad_key_weight,
        grad_value_weight,
    )


def solution(mesh):
    return jax.shard_map(
        on_device,
        mesh=mesh,
        in_specs=(
            P(("dp", "tensor"), None),
            P("dp", "tensor"),
            P("dp", None),
            P(),
            P(("dp", "tensor"), None),
            P(("dp", "tensor"), None),
            P(),
            P(),
            P(),
            P(),
            P(),
            P(),
            P(),
            P(),
            P(None, "dp", "tensor"),
            P("tensor", "dp"),
            P("dp", "tensor"),
            P("tensor", "dp"),
        ),
        out_specs=(
            P(("dp", "tensor"), None),
            P(),
            P(("dp", "tensor"), None),
            P("dp", "tensor"),
            P(),
            P(),
            P(),
            P(),
            P(),
            P(),
            P(),
            P(),
            P(),
            P(None, "dp", "tensor"),
            P("tensor", "dp"),
            P("dp", "tensor"),
            P("tensor", "dp"),
        ),
        check_vma=False,
    )
```

profile of v0, /device:TPU:0, one launch (start us, length us, event | category | flops | bytes accessed | tf_op | source)
XLA Modules:
  0.0 1059.5 jit_solution(9933025152362144689)
XLA Ops:
  17.7 20.6 %all-gather.9.cloned.1.call-done = bf16[512,1024]{1,0:T(8,128)(2,1)} async-done(((bf16[256,1024]{1,0:T(8,128)(2,1)}), bf16[512,1024]{1,0:T(8,128)(2,1)}) %all-gather.9.cloned.1.call-update) | async-done | bytes 1048592 | tf_op jit(solution)/shard_map/all_gather | solution.py:547
  50.3 35.6 %all-gather.11.cloned.1.call-done = bf16[3,1024,512]{2,1,0:T(8,128)(2,1)} async-done(((bf16[3,64,512]{2,1,0:T(8,128)(2,1)}), bf16[3,1024,512]{2,1,0:T(8,128)(2,1)}) %all-gather.11.cloned.1.call-update) | async-done | bytes 3145744 | tf_op jit(solution)/shard_map/all_gather | solution.py:538
  93.3 33.9 %mixer_forward.1 = (bf16[512,512]{1,0:T(8,128)(2,1)S(1)}, f32[512,512]{1,0:T(8,128)S(1)}, f32[512,512]{1,0:T(8,128)S(1)}, f32[8,4,128,128]{3,2,1,0:T(8,128)}, f3...) custom-call(f32[512,512]{1,0:T(8,128)S(1)} %fusion.30.r_ref, ...), custom_call_target="tpu_custom_call" | custom-call | flops 7650410496 | bytes 23068672 | tf_op jit(solution)/shard_map/mixer_forward/pallas_call | solution.py:439
  133.6 30.7 %reduce-scatter.10.cloned.1.call-done = f32[256,1024]{1,0:T(8,128)} async-done(((f32[512,1024]{1,0:T(8,128)}), f32[256,1024]{1,0:T(8,128)}) %reduce-scatter.10.cloned.1.call-update) | async-done | bytes 1048592 | tf_op jit(solution)/shard_map/reduce_scatter | solution.py:592
  168.6 19.9 %all-gather.15.cloned.1.call-done = bf16[512,1024]{1,0:T(8,128)(2,1)} async-done(((bf16[256,1024]{1,0:T(8,128)(2,1)}), bf16[512,1024]{1,0:T(8,128)(2,1)}) %all-gather.15.cloned.1.call-update) | async-done | bytes 1048592 | tf_op jit(solution)/shard_map/all_gather | solution.py:599
  193.0 48.5 %all-gather.17.cloned.1.call-done = bf16[1024,2048]{1,0:T(8,128)(2,1)} async-done(((bf16[64,2048]{1,0:T(8,128)(2,1)}), bf16[1024,2048]{1,0:T(8,128)(2,1)}) %all-gather.17.cloned.1.call-update) | async-done | bytes 4194320 | tf_op jit(solution)/shard_map/all_gather | solution.py:540
  241.6 6.9 fusion.101
  248.5 44.5 %all-gather.19.cloned.1.call-done = bf16[2048,1024]{0,1:T(8,128)(2,1)} async-done(((bf16[2048,64]{0,1:T(8,128)(2,1)}), bf16[2048,1024]{0,1:T(8,128)(2,1)}) %all-gather.19.cloned.1.call-update) | async-done | bytes 4194320 | tf_op jit(solution)/shard_map/all_gather | solution.py:541
  293.0 7.2 fusion.36
  304.5 26.2 %reduce-scatter.12.cloned.1.call-done = f32[256,1024]{1,0:T(8,128)} async-done(((f32[512,1024]{1,0:T(8,128)}), f32[256,1024]{1,0:T(8,128)}) %reduce-scatter.12.cloned.1.call-update) | async-done | bytes 1048592 | tf_op jit(solution)/shard_map/reduce_scatter | solution.py:607
  333.5 21.3 %all-gather.21.cloned.1.call-done = bf16[512,1024]{1,0:T(8,128)(2,1)} async-done(((bf16[256,1024]{1,0:T(8,128)(2,1)}), bf16[512,1024]{1,0:T(8,128)(2,1)}) %all-gather.21.cloned.1.call-update) | async-done | bytes 1048592 | tf_op jit(solution)/shard_map/all_gather | solution.py:618
  354.8 6.3 multiply_convert_fusion
  369.4 31.9 %reduce-scatter.14.cloned.1.call-done = f32[256,1024]{1,0:T(8,128)} async-done(((f32[512,1024]{1,0:T(8,128)}), f32[256,1024]{1,0:T(8,128)}) %reduce-scatter.14.cloned.1.call-update) | async-done | bytes 1048592 | tf_op jit(solution)/shard_map/reduce_scatter | solution.py:626
  407.6 21.2 %all-gather.23.cloned.1.call-done = bf16[512,1024]{1,0:T(8,128)(2,1)} async-done(((bf16[256,1024]{1,0:T(8,128)(2,1)}), bf16[512,1024]{1,0:T(8,128)(2,1)}) %all-gather.23.cloned.1.call-update) | async-done | bytes 1048592 | tf_op jit(solution)/shard_map/all_gather | solution.py:629
  431.8 38.2 %mixer_backward.1 = (bf16[512,512]{1,0:T(8,128)(2,1)S(1)}, bf16[512,512]{1,0:T(8,128)(2,1)S(1)}, bf16[512,512]{1,0:T(8,128)(2,1)S(1)}, bf16[512,512]{1,0:T(8,128...) custom-call(f32[512,512]{1,0:T(8,128)S(1)} %fusion.103.dz_ref, ...), custom_call_target="tpu_custom_call" | custom-call | flops 6039797760 | bytes 29360128 | tf_op jit(solution)/shard_map/mixer_backward/pallas_call | solution.py:465
  480.9 7.1 reduce-scatter.16.cloned.1.call-done
  513.3 7.9 fusion.35
  522.4 7.3 fusion.107
  542.1 41.6 %all-reduce.10 = (f32[]{:T(128)}, f32[2,1024]{1,0:T(2,128)}, f32[2,1024]{1,0:T(2,128)}, f32[7,1024]{1,0:T(8,128)S(1)}, f32[1024]{0:T(1024)}, /*index=5*/f32[3,1024]{1,0:T(4,128)}, f32[4,1024]{1,0:T(4,128)}) all-reduce(f32[]{:T(128)S(6)} %div.53, ...), channel_id=1, replica_groups=mesh['dp'=16,'tensor'=2] {'dp','tensor'}, use_global_device_ids=true, to_apply=%region_8.0 | all-reduce | flops 19457 | bytes 155656 | tf_op jit(solution)/shard_map/psum | solution.py:760
  587.9 88.2 %all-reduce.9.cloned.1.call-done = (f32[1024,288]{0,1:T(8,128)}, f32[288,1024]{1,0:T(8,128)}) async-done(((f32[1024,288]{0,1:T(8,128)}, f32[288,1024]{1,0:T(8,128)}), (f32[1024,288]{0,1:T(8,128)}, f32[288,1024]{1,0:T(8,128)})) %all-reduce.9.cloned.1.call-update) | async-done | bytes 2359312 | tf_op jit(solution)/shard_map/psum | solution.py:760
  676.1 64.7 %reduce-scatter.22.cloned.1.call-done = f32[512,64]{0,1:T(8,128)} async-done(((f32[512,1024]{0,1:T(8,128)}), f32[512,64]{0,1:T(8,128)}) %reduce-scatter.22.cloned.1.call-update) | async-done | bytes 131088 | tf_op jit(solution)/shard_map/reduce_scatter | solution.py:776
  740.8 108.7 %reduce-scatter.26.cloned.1.call-done = f32[2048,64]{0,1:T(8,128)} async-done(((f32[2048,1024]{0,1:T(8,128)}), f32[2048,64]{0,1:T(8,128)}) %reduce-scatter.26.cloned.1.call-update) | async-done | bytes 524304 | tf_op jit(solution)/shard_map/reduce_scatter | solution.py:778
  849.4 109.4 %reduce-scatter.24.cloned.1.call-done = f32[64,2048]{1,0:T(8,128)} async-done(((f32[1024,2048]{1,0:T(8,128)}), f32[64,2048]{1,0:T(8,128)}) %reduce-scatter.24.cloned.1.call-update) | async-done | bytes 524304 | tf_op jit(solution)/shard_map/reduce_scatter | solution.py:777
  958.9 89.9 %reduce-scatter.20.cloned.1.call-done = f32[3,64,512]{2,1,0:T(8,128)} async-done(((f32[3,1024,512]{2,1,0:T(8,128)}), f32[3,64,512]{2,1,0:T(8,128)}) %reduce-scatter.20.cloned.1.call-update) | async-done | bytes 393232 | tf_op jit(solution)/shard_map/reduce_scatter | solution.py:775
  (366 shorter events, 124.5 us)
Async XLA Ops:
  7.3 31.1 %all-gather.9.cloned.1.call-start = ((), (), s32[]{:S(2)}) async-start(), calls=%async_computation.9 | async-start | bytes 1572864 | tf_op jit(solution)/shard_map/all_gather | solution.py:547
  14.2 71.7 %all-gather.11.cloned.1.call-start = ((), (), s32[]{:S(2)}) async-start(), calls=%async_computation.10 | async-start | bytes 3342336 | tf_op jit(solution)/shard_map/all_gather | solution.py:538
  14.9 115.2 %all-gather.13.cloned.1.call-start = ((), (), s32[]{:S(2)}) async-start(), calls=%async_computation.11 | async-start | bytes 1114112 | tf_op jit(solution)/shard_map/all_gather | solution.py:539
  15.7 148.6 %reduce-scatter.10.cloned.1.call-start = ((), (), s32[]{:S(2)}) async-start(), calls=%async_computation.12 | async-start | bytes 3145728 | tf_op jit(solution)/shard_map/reduce_scatter | solution.py:592
  17.0 173.1 %copy-start.70 = (f32[1,1024]{1,0:T(1,128)}, f32[1,1024]{1,0:T(1,128)S(1)}, u32[]{:S(2)}) copy-start(f32[1,1024]{1,0:T(1,128)S(1)} %get-tuple-element.105) | copy-start | bytes 12292
  46.4 39.5 %copy-start.24 = (bf16[512,1024]{1,0:T(8,128)(2,1)S(1)}, bf16[512,1024]{1,0:T(8,128)(2,1)}, u32[]{:S(2)}) copy-start(bf16[512,1024]{1,0:T(8,128)(2,1)} %copy-done.23) | copy-start | bytes 3145732
  133.5 55.0 %all-gather.15.cloned.1.call-start = ((), (), s32[]{:S(2)}) async-start(), calls=%async_computation.13 | async-start | bytes 1572864 | tf_op jit(solution)/shard_map/all_gather | solution.py:599
  167.1 74.5 %all-gather.17.cloned.1.call-start = ((), (), s32[]{:S(2)}) async-start(), calls=%async_computation.14 | async-start | bytes 4456448 | tf_op jit(solution)/shard_map/all_gather | solution.py:540
  167.7 125.4 %all-gather.19.cloned.1.call-start = ((), (), s32[]{:S(2)}) async-start(), calls=%async_computation.15 | async-start | bytes 4456448 | tf_op jit(solution)/shard_map/all_gather | solution.py:541
  168.4 162.3 %reduce-scatter.12.cloned.1.call-start = ((), (), s32[]{:S(2)}) async-start(), calls=%async_computation.16 | async-start | bytes 3145728 | tf_op jit(solution)/shard_map/reduce_scatter | solution.py:607
  300.2 54.6 %all-gather.21.cloned.1.call-start = ((), (), s32[]{:S(2)}) async-start(), calls=%async_computation.17 | async-start | bytes 1572864 | tf_op jit(solution)/shard_map/all_gather | solution.py:618
  333.4 67.9 %reduce-scatter.14.cloned.1.call-start = ((), (), s32[]{:S(2)}) async-start(), calls=%async_computation.18 | async-start | bytes 3145728 | tf_op jit(solution)/shard_map/reduce_scatter | solution.py:626
  369.3 59.5 %all-gather.23.cloned.1.call-start = ((), (), s32[]{:S(2)}) async-start(), calls=%async_computation.19 | async-start | bytes 1572864 | tf_op jit(solution)/shard_map/all_gather | solution.py:629
  407.4 80.6 %reduce-scatter.16.cloned.1.call-start = ((), (), s32[]{:S(2)}) async-start(), calls=%async_computation.20 | async-start | bytes 884736 | tf_op jit(solution)/shard_map/reduce_scatter | solution.py:686
  431.8 39.0 %copy-start.46 = (f32[512,128]{0,1:T(8,128)S(1)}, f32[512,128]{0,1:T(8,128)}, u32[]{:S(2)}) copy-start(f32[512,128]{0,1:T(8,128)} %copy-done.45) | copy-start | bytes 786436
  472.6 66.1 %reduce-scatter.18.cloned.1.call-start = ((), (), s32[]{:S(2)}) async-start(), calls=%async_computation.21 | async-start | bytes 3145728 | tf_op jit(solution)/shard_map/reduce_scatter | solution.py:746
  501.3 174.8 %all-reduce.9.cloned.1.call-start = ((), (), s32[]{:S(2)}) async-start(), calls=%async_computation.26 | async-start | bytes 4718592 | tf_op jit(solution)/shard_map/psum | solution.py:760
  508.6 232.1 %reduce-scatter.22.cloned.1.call-start = ((), (), s32[]{:S(2)}) async-start(), calls=%async_computation.23 | async-start | bytes 2228224 | tf_op jit(solution)/shard_map/reduce_scatter | solution.py:776
  512.1 337.4 %reduce-scatter.26.cloned.1.call-start = ((), (), s32[]{:S(2)}) async-start(), calls=%async_computation.25 | async-start | bytes 8912896 | tf_op jit(solution)/shard_map/reduce_scatter | solution.py:778
  521.2 437.7 %reduce-scatter.24.cloned.1.call-start = ((), (), s32[]{:S(2)}) async-start(), calls=%async_computation.24 | async-start | bytes 8912896 | tf_op jit(solution)/shard_map/reduce_scatter | solution.py:777
  529.7 519.0 %reduce-scatter.20.cloned.1.call-start = ((), (), s32[]{:S(2)}) async-start(), calls=%async_computation.22 | async-start | bytes 6684672 | tf_op jit(solution)/shard_map/reduce_scatter | solution.py:775
  537.5 47.4 %copy-start.28 = (f32[256,1024]{1,0:T(8,128)S(1)}, f32[256,1024]{1,0:T(8,128)}, u32[]{:S(2)}) copy-start(f32[256,1024]{1,0:T(8,128)} %copy-done.27) | copy-start | bytes 3145732
  537.5 47.4 %copy-start.97 = (f32[256]{0:T(256)S(1)}, f32[256]{0:T(256)}, u32[]{:S(2)}) copy-start(f32[256]{0:T(256)} %copy-done.96) | copy-start | bytes 3076
  676.1 375.1 %copy-start.55 = (f32[288,1024]{1,0:T(8,128)S(1)}, f32[288,1024]{1,0:T(8,128)}, u32[]{:S(2)}) copy-start(f32[288,1024]{1,0:T(8,128)} %get-tuple-element.127) | copy-start | bytes 3538948
  (99 other events, 769.3 us)
Sparse Core Ops, SparseCore 0:
  14.3 23.9 all-gather.8
  40.5 45.3 all-gather.10
  88.1 36.7 all-gather.12
  133.7 30.6 reduce-scatter.9
  167.2 21.3 all-gather.14
  190.8 50.7 all-gather.16
  243.9 49.0 all-gather.18
  300.3 30.3 reduce-scatter.11
  333.5 21.2 all-gather.20
  369.4 31.8 reduce-scatter.13
  407.5 21.2 all-gather.22
  472.7 15.2 reduce-scatter.15
  501.4 31.8 reduce-scatter.17
  540.4 135.6 all-reduce.8
  680.3 60.4 reduce-scatter.21
  745.8 103.5 reduce-scatter.25
  854.5 104.3 reduce-scatter.23
  963.7 84.9 reduce-scatter.19
where the time goes:
time: 1070 us; the launch traced here: 1060 us
  waiting for transfers between devices  771 us (72%)
  matrix products  80 us (7%)
  Pallas kernels  72 us (7%)
  other arithmetic  44.9 us (4%)
  blocking collectives  41.6 us (4%)
  local copies, waits for them, and re-layouts  31 us (3%)
  between operations  17.4 us (2%)
    reduce_scatter x1, waiting for transfers between devices, on_device(): lax.psum_scatter(grad_key_part, 'dp', scatter_dimension=0, tiled=True)  109 us
    reduce_scatter x1, waiting for transfers between devices, on_device(): lax.psum_scatter(grad_value_part, 'dp', scatter_dimension=1, tiled=True)  109 us
    reduce_scatter x1, waiting for transfers between devices, on_device(): lax.psum_scatter(grad_rkv_part, 'dp', scatter_dimension=1, tiled=True)  89.9 us
    psum x1, waiting for transfers between devices, on_device(): lax.psum((small_terms[0], small_terms[1], small_terms[2], small_terms[3],...  88.2 us
    reduce_scatter x1, waiting for transfers between devices, on_device(): lax.psum_scatter(grad_out_part, 'dp', scatter_dimension=1, tiled=True)  64.7 us
    all_gather x1, waiting for transfers between devices, on_device(): lax.all_gather(channel_key_weight, 'dp', axis=0, tiled=True)  48.5 us
    all_gather x1, waiting for transfers between devices, on_device(): lax.all_gather(channel_value_weight, 'dp', axis=1, tiled=True)  44.5 us
    psum x1, blocking collectives, on_device(): lax.psum((small_terms[0], small_terms[1], small_terms[2], small_terms[3],...  41.6 us
  transfers between devices with their start and end apart: 18, of which 16 were waited for; matrix products, arithmetic and copies ran while one was open for 8% of the time, Pallas kernels for 3%

commit v1 on v0

v1 whole, which is shorter than its diff:
```python
import jax
import jax.numpy as jnp
from jax import lax
from jax.experimental import pallas as pl
from jax.experimental.pallas import tpu as pltpu
from jax.sharding import PartitionSpec as P

HEAD_SIZE = 64
CHUNK = 64
PAIR = 2 * HEAD_SIZE
BF = jnp.bfloat16
F32 = jnp.float32
DECAY_SCALE = 0.6065306597126334
DECAY_MAP_RANK = 64
RATE_MAP_RANK = 64
VALUE_MIX_RANK = 32


def matrix_multiply(left, right):
    return jnp.dot(left, right, preferred_element_type=jnp.float32)


def matmul_tn(left, right):
    return lax.dot_general(
        left, right, (((0,), (0,)), ((), ())), preferred_element_type=jnp.float32
    )


def matrix_multiply_transposed(left, right):
    return lax.dot_general(
        left, right, (((1,), (1,)), ((), ())), preferred_element_type=jnp.float32
    )


def shift_down(row_data, retain_mask):
    return jnp.concatenate([jnp.zeros_like(row_data[:1]), row_data[:-1]], 0) * retain_mask[:, None]


def shift_up(row_data, retain_mask):
    moved = row_data * retain_mask[:, None]
    return jnp.concatenate([moved[1:], jnp.zeros_like(moved[:1])], 0)


def place_cols(col_block, total_cols, first_col):
    zeros_full = jnp.zeros(col_block.shape[:-1] + (total_cols,), jnp.float32)
    return lax.dynamic_update_slice_in_dim(zeros_full, col_block, first_col, col_block.ndim - 1)


NN = (((1,), (0,)), ((), ()))
NT = (((1,), (1,)), ((), ()))
TN = (((0,), (0,)), ((), ()))


def split(x, terms=2):
    hi = x.astype(BF)
    if terms == 1:
        return (hi,)
    return (hi, (x - hi.astype(F32)).astype(BF))


def mm(a, b, dims):
    out = lax.dot_general(a[0], b[0], dims, preferred_element_type=F32)
    if len(b) > 1:
        out = out + lax.dot_general(a[0], b[1], dims, preferred_element_type=F32)
    if len(a) > 1:
        out = out + lax.dot_general(a[1], b[0], dims, preferred_element_type=F32)
    return out


def rows_of(*parts):
    return tuple(jnp.concatenate(terms, 0) for terms in zip(*parts))


def cols_of(*parts):
    return tuple(jnp.concatenate(terms, 1) for terms in zip(*parts))


def spread(parts, left, right):
    return tuple(jnp.concatenate([x * left, x * right], 0) for x in parts)


def chunk_masks(gcol, aux):
    size = 2 * CHUNK
    row = lax.broadcasted_iota(jnp.int32, (size, size), 0)
    lane = lax.broadcasted_iota(jnp.int32, (size, size), 1)
    t_row, t_lane = row & (CHUNK - 1), lane & (CHUNK - 1)
    same_head = (row >= CHUNK) == (lane >= CHUNK)
    g_row = jnp.concatenate([gcol, gcol], 0)
    linked = (g_row == aux[0:1, :]) & same_head
    strict = linked & (t_row > t_lane)
    upto = linked & (t_row >= t_lane)
    from_start = (gcol == aux[2:3, :]).astype(F32)
    to_end = (gcol == aux[1:2, :]).astype(F32)
    end_clear = (aux[1:2, :] == aux[2:3, :]).astype(F32)
    return row, lane, t_row, t_lane, strict, upto, from_start, to_end, end_clear


def head_sum(x, ones):
    return mm(split(x), (ones,), NN)


def lane_masks():
    lane = lax.broadcasted_iota(jnp.int32, (1, PAIR), 1)
    left = (lane < HEAD_SIZE).astype(F32)
    return left.astype(BF), (1.0 - left).astype(BF), left


def head_ones():
    row = lax.broadcasted_iota(jnp.int32, (PAIR, PAIR), 0)
    lane = lax.broadcasted_iota(jnp.int32, (PAIR, PAIR), 1)
    return ((row >= HEAD_SIZE) == (lane >= HEAD_SIZE)).astype(F32).astype(BF)


def lower_ones():
    row = lax.broadcasted_iota(jnp.int32, (CHUNK, CHUNK), 0)
    lane = lax.broadcasted_iota(jnp.int32, (CHUNK, CHUNK), 1)
    return (row >= lane).astype(F32).astype(BF)


def split3(x):
    hi = x.astype(BF)
    rest = x - hi.astype(F32)
    mid = rest.astype(BF)
    return (hi, mid, (rest - mid.astype(F32)).astype(BF))


def ones_times(ones, x, dims):
    total = None
    for term in split3(x):
        part = lax.dot_general(ones, term, dims, preferred_element_type=F32)
        total = part if total is None else total + part
    return total


def sigmoid(x):
    return jax.nn.sigmoid(x)


def low_cols(ref, index, cols):
    start = index * (ref.shape[1] // 4)
    return slice(start + cols.start, start + cols.stop)


def pair_values(refs, par, cols, ones):
    r_ref, kp_ref, vp_ref, low_ref, vf_ref = refs
    out = {}
    r, kp, vp = r_ref[:, cols], kp_ref[:, cols], vp_ref[:, cols]
    vf = vf_ref[:, cols].astype(F32)
    a = sigmoid(par[4:5] + low_ref[:, low_cols(low_ref, 1, cols)])
    s = sigmoid(par[5:6] + low_ref[:, low_cols(low_ref, 2, cols)])
    v = vp + (vf - vp) * s
    sg = sigmoid(par[0:1] + low_ref[:, low_cols(low_ref, 0, cols)])
    ld = -DECAY_SCALE * sg
    u = kp * par[1:2]
    inv = lax.rsqrt(head_sum(u * u, ones) + 1e-06)
    kk = u * inv
    k = kp * (1.0 + (a - 1.0) * par[2:3])
    out.update(r=r, kp=kp, vp=vp, vf=vf, a=a, s=s, v=v, sg=sg, ld=ld, inv=inv, kk=kk, k=k)
    return out


def chunk_values(w, lower, from_start, to_end, end_clear):
    inc = ones_times(lower, w["ld"], NN)
    exc = inc - w["ld"]
    last = inc[CHUNK - 1 : CHUNK, :]
    w["e_inc"] = jnp.exp(inc)
    w["e_exc"] = jnp.exp(exc)
    w["e_neg"] = jnp.exp(-inc)
    w["carry"] = jnp.exp(last - inc) * to_end
    w["finish"] = jnp.exp(last) * end_clear
    w["b"] = w["kk"] * w["a"]
    w["kappa"] = w["kk"] * w["e_exc"]
    w["rho"] = w["r"] * w["e_inc"]
    w["key_hat"] = w["k"] * w["e_neg"]
    w["take_hat"] = w["b"] * w["e_neg"]
    w["k_end"] = w["k"] * w["carry"]
    w["b_end"] = w["b"] * w["carry"]
    w["kappa0"] = w["kappa"] * from_start
    w["rho0"] = w["rho"] * from_start


def forward_kernel(
    r_ref, kp_ref, vp_ref, low_ref, vf_ref, par_ref, gcol_ref, aux_ref,
    z_ref, y_ref, q_ref, t_ref, akk_ref, ark_ref, arb_ref, s0_ref, state,
):
    pairs = r_ref.shape[1] // PAIR

    @pl.when(pl.program_id(0) == 0)
    def _():
        state[...] = jnp.zeros_like(state)

    masks = chunk_masks(gcol_ref[...], aux_ref[0])
    row, lane, t_row, t_lane, strict, upto, from_start, to_end, end_clear = masks
    left, right, left_f = lane_masks()
    ones = head_ones()
    lower = lower_ones()
    eye = (row == lane).astype(F32)
    in8 = (t_row >> 3) == (t_lane >> 3)
    levels = []
    for bits in (3, 4, 5):
        levels.append(((t_row >> (bits + 1)) == (t_lane >> (bits + 1))) & ((t_row >> bits) != (t_lane >> bits)))
    group = range(pairs)
    cols = [slice(p * PAIR, (p + 1) * PAIR) for p in group]
    refs = (r_ref, kp_ref, vp_ref, low_ref, vf_ref)
    pars = [par_ref[:, cols[p]] for p in group]
    w = [pair_values(refs, pars[p], cols[p], ones) for p in group]
    for p in group:
        chunk_values(w[p], lower, from_start, to_end, end_clear)
    akk, akb, ark, arb = [], [], [], []
    for p in group:
        x = w[p]
        rows = rows_of(spread(split(x["kappa"]), left, right), spread(split(x["rho"]), left, right))
        keys = rows_of(spread(split(x["key_hat"]), left, right), spread(split(x["take_hat"]), left, right))
        scores = mm(rows, keys, NT)
        n = 2 * CHUNK
        akk.append(jnp.where(strict, scores[:n, :n], 0.0))
        akb.append(jnp.where(strict, scores[:n, n:], 0.0))
        ark.append(jnp.where(upto, scores[n:, :n], 0.0))
        arb.append(jnp.where(upto, scores[n:, n:], 0.0))
    neg = [jnp.where(in8, -akb[p], 0.0) for p in group]
    neg_s = [split(x) for x in neg]
    two = [mm(x, x, NN) for x in neg_s]
    two_s = [split(x) for x in two]
    both = [mm(rows_of(neg_s[p], two_s[p]), two_s[p], NN) for p in group]
    n = 2 * CHUNK
    low = [neg[p] + two[p] + both[p][:n] for p in group]
    four = [both[p][n:] for p in group]
    inv = [eye + low[p] + four[p] + mm(split(low[p]), split(four[p]), NN) for p in group]
    for level in levels:
        inv_s = [split(x) for x in inv]
        mid = [mm(split(jnp.where(level, akb[p], 0.0)), inv_s[p], NN) for p in group]
        inv = [inv[p] - mm(inv_s[p], split(mid[p]), NN) for p in group]
    inv_s = [split(x) for x in inv]
    v_s = [spread(split(w[p]["v"]), left, right) for p in group]
    akk_v = [mm(split(akk[p]), v_s[p], NN) for p in group]
    s0 = [state[p] for p in group]
    carried = [
        mm(
            rows_of(spread(split(w[p]["kappa0"]), left, right), spread(split(w[p]["rho0"]), left, right)),
            split(s0[p]),
            NT,
        )
        for p in group
    ]
    q = [mm(inv_s[p], split(carried[p][:n] + akk_v[p]), NN) for p in group]
    q_s = [split(x) for x in q]
    y2 = [
        carried[p][n:] + mm(cols_of(split(ark[p]), split(-arb[p])), rows_of(v_s[p], q_s[p]), NN)
        for p in group
    ]
    for p in group:
        x = w[p]
        ends = rows_of(spread(split(x["k_end"]), left, right), spread(split(-x["b_end"]), left, right))
        state[p] = s0[p] * x["finish"] + mm(rows_of(v_s[p], q_s[p]), ends, TN)
        y = y2[p][:CHUNK] + y2[p][CHUNK:]
        y_ref[:, cols[p]] = y
        q_ref[:, cols[p]] = q[p][:CHUNK] + q[p][CHUNK:]
        t_ref[0, p] = inv[p]
        akk_ref[0, p] = akk[p]
        ark_ref[0, p] = ark[p]
        arb_ref[0, p] = arb[p]
        s0_ref[0, p] = s0[p]
        par = pars[p]
        centred = y - head_sum(y, ones) * (1.0 / HEAD_SIZE)
        var = head_sum(centred * centred, ones) * (1.0 / HEAD_SIZE)
        normed = centred * lax.rsqrt(var + HEAD_SIZE * 0.01)
        bonus = head_sum(x["r"] * x["k"] * par[6:7], ones)
        z = (normed * par[3:4] + par[7:8] + bonus * x["v"]) * low_ref[:, low_cols(low_ref, 3, cols[p])]
        z_ref[:, cols[p]] = z.astype(z_ref.dtype)


def backward_kernel(
    dz_ref, r_ref, kp_ref, vp_ref, low_ref, vf_ref, par_ref, gcol_ref, aux_ref,
    y_ref, q_ref, t_ref, akk_ref, ark_ref, arb_ref, s0_ref,
    dr_ref, dkp_ref, dvp_ref, dlow_ref, dvf_ref, dpar_ref, state,
):
    pairs = r_ref.shape[1] // PAIR
    n = 2 * CHUNK

    @pl.when(pl.program_id(0) == 0)
    def _():
        state[...] = jnp.zeros_like(state)
        dpar_ref[...] = jnp.zeros_like(dpar_ref)

    masks = chunk_masks(gcol_ref[...], aux_ref[0])
    row, lane, t_row, t_lane, strict, upto, from_start, to_end, end_clear = masks
    left, right, left_f = lane_masks()
    ones = head_ones()
    lower = lower_ones()
    last_row = (lax.broadcasted_iota(jnp.int32, (CHUNK, 1), 0) == CHUNK - 1).astype(F32)
    group = range(pairs)
    cols = [slice(p * PAIR, (p + 1) * PAIR) for p in group]
    refs = (r_ref, kp_ref, vp_ref, low_ref, vf_ref)
    pars = [par_ref[:, cols[p]] for p in group]
    w = [pair_values(refs, pars[p], cols[p], ones) for p in group]
    scale = 1.0 / HEAD_SIZE
    for p in group:
        x, par = w[p], pars[p]
        chunk_values(x, lower, from_start, to_end, end_clear)
        y = y_ref[:, cols[p]]
        centred = y - head_sum(y, ones) * scale
        var = head_sum(centred * centred, ones) * scale
        istd = lax.rsqrt(var + HEAD_SIZE * 0.01)
        normed = centred * istd
        rk = x["r"] * x["k"]
        bonus = head_sum(rk * par[6:7], ones)
        dz = dz_ref[:, cols[p]]
        dlow_ref[:, low_cols(low_ref, 3, cols[p])] = (dz * (normed * par[3:4] + par[7:8] + bonus * x["v"])).astype(BF)
        do = dz * low_ref[:, low_cols(low_ref, 3, cols[p])]
        dbonus = head_sum(do * x["v"], ones)
        x["dv"] = do * bonus
        x["dr"] = dbonus * x["k"] * par[6:7]
        x["dk"] = dbonus * x["r"] * par[6:7]
        dn = do * par[3:4]
        x["dy"] = istd * (dn - head_sum(dn, ones) * scale - normed * (head_sum(dn * normed, ones) * scale))
        x["g2"] = jnp.sum(do * normed, 0, keepdims=True)
        x["b3"] = jnp.sum(do, 0, keepdims=True)
        x["b2"] = jnp.sum(dbonus * rk, 0, keepdims=True)
    dy_s = [spread(split(w[p]["dy"]), left, right) for p in group]
    v_s = [spread(split(w[p]["v"]), left, right) for p in group]
    q_s = [spread(split(q_ref[:, cols[p]]), left, right) for p in group]
    ds = [state[p] for p in group]
    ds_s = [split(ds[p]) for p in group]
    kend_s = [spread(split(w[p]["k_end"]), left, right) for p in group]
    bend_s = [spread(split(w[p]["b_end"]), left, right) for p in group]
    from_end = [mm(rows_of(kend_s[p], bend_s[p]), ds_s[p], NT) for p in group]
    dq = [-(mm(split(arb_ref[0, p]), dy_s[p], TN) + from_end[p][n:]) for p in group]
    du = [mm(split(t_ref[0, p]), split(dq[p]), TN) for p in group]
    du_s = [split(du[p]) for p in group]
    uy_s = [rows_of(du_s[p], dy_s[p]) for p in group]
    s0 = [s0_ref[0, p] for p in group]
    kappa_s = [spread(split(w[p]["kappa"]), left, right) for p in group]
    rho_s = [spread(split(w[p]["rho"]), left, right) for p in group]
    for p in group:
        x = w[p]
        start = rows_of(spread(split(x["kappa0"]), left, right), spread(split(x["rho0"]), left, right))
        state[p] = ds[p] * x["finish"] + mm(uy_s[p], start, TN)
    dv2 = [
        from_end[p][:n] + mm(rows_of(split(akk_ref[0, p]), split(ark_ref[0, p])), uy_s[p], TN)
        for p in group
    ]
    start_grad = [mm(uy_s[p], split(s0[p]), NN) for p in group]
    end_grad = [mm(rows_of(v_s[p], q_s[p]), ds_s[p], NN) for p in group]
    vq_s = [rows_of(v_s[p], tuple(-t for t in q_s[p])) for p in group]
    raw = [mm(uy_s[p], vq_s[p], NT) for p in group]
    da_s = []
    for p in group:
        top = jnp.where(jnp.concatenate([strict, strict], 1), raw[p][:n], 0.0)
        bottom = jnp.where(jnp.concatenate([upto, upto], 1), raw[p][n:], 0.0)
        da_s.append(split(jnp.concatenate([top, bottom], 0)))
    row_grad = [
        mm(
            da_s[p],
            rows_of(spread(split(w[p]["key_hat"]), left, right), spread(split(w[p]["take_hat"]), left, right)),
            NN,
        )
        for p in group
    ]
    col_grad = [mm(da_s[p], rows_of(kappa_s[p], rho_s[p]), TN) for p in group]

    def fold(z):
        return z[:CHUNK] + z[CHUNK:n], z[n : n + CHUNK] + z[n + CHUNK :]

    for p in group:
        x, par = w[p], pars[p]
        dkappa0, drho0 = fold(start_grad[p])
        dkend, dbend = fold(end_grad[p])
        dbend = -dbend
        dkappa, drho = fold(row_grad[p])
        dkey, dtake = fold(col_grad[p])
        dkappa = dkappa + dkappa0 * from_start
        drho = drho + drho0 * from_start
        dv = x["dv"] + dv2[p][:CHUNK] + dv2[p][CHUNK:]
        dr = x["dr"] + drho * x["e_inc"]
        dk = x["dk"] + dkey * x["e_neg"] + dkend * x["carry"]
        db = dtake * x["e_neg"] + dbend * x["carry"]
        dkk = dkappa * x["e_exc"] + db * x["a"]
        da = db * x["kk"]
        dexc = dkappa * x["kappa"]
        dends = dkend * x["k_end"] + dbend * x["b_end"]
        dinc = drho * x["rho"] - dkey * x["key_hat"] - dtake * x["take_hat"] - dends
        dlast = jnp.sum(dends, 0, keepdims=True) + jnp.sum(s0[p] * ds[p], 0, keepdims=True) * x["finish"]
        dld = ones_times(lower, dinc + dexc + last_row * dlast, TN) - dexc
        dkp = dk * (1.0 + (x["a"] - 1.0) * par[2:3])
        da = da + dk * x["kp"] * par[2:3]
        g1 = jnp.sum(dk * x["kp"] * (x["a"] - 1.0), 0, keepdims=True)
        dunit = x["inv"] * (dkk - x["kk"] * head_sum(dkk * x["kk"], ones))
        dkp = dkp + dunit * par[1:2]
        g0 = jnp.sum(dunit * x["kp"], 0, keepdims=True)
        dev = dv * (x["vf"] - x["vp"]) * x["s"] * (1.0 - x["s"])
        dea = da * x["a"] * (1.0 - x["a"])
        dew = dld * (-DECAY_SCALE) * x["sg"] * (1.0 - x["sg"])
        dr_ref[:, cols[p]] = dr.astype(BF)
        dkp_ref[:, cols[p]] = dkp.astype(BF)
        dvp_ref[:, cols[p]] = (dv * (1.0 - x["s"])).astype(BF)
        dvf_ref[:, cols[p]] = dv * x["s"]
        dlow_ref[:, low_cols(low_ref, 0, cols[p])] = dew.astype(BF)
        dlow_ref[:, low_cols(low_ref, 1, cols[p])] = dea.astype(BF)
        dlow_ref[:, low_cols(low_ref, 2, cols[p])] = dev.astype(BF)
        dpar_ref[:, cols[p]] += jnp.concatenate(
            [
                jnp.sum(dew, 0, keepdims=True),
                g0,
                g1,
                x["g2"],
                jnp.sum(dea, 0, keepdims=True),
                jnp.sum(dev, 0, keepdims=True),
                x["b2"],
                x["b3"],
            ],
            0,
        )


def token_spec(cols, order):
    return pl.BlockSpec((CHUNK, cols), lambda i: (order(i), 0))


def square_spec(pairs, order):
    return pl.BlockSpec((1, pairs, PAIR, PAIR), lambda i: (order(i), 0, 0, 0))


def mixer_specs(cols, order):
    tok = token_spec(cols, order)
    return [tok, tok, tok, token_spec(4 * cols, order), tok] + [
        pl.BlockSpec((8, cols), lambda i: (0, 0)),
        pl.BlockSpec((CHUNK, 1), lambda i: (order(i), 0)),
        pl.BlockSpec((1, 8, PAIR), lambda i: (order(i), 0, 0)),
    ]


def mixer_forward(r, *rest):
    tokens, cols = r.shape
    steps, pairs = tokens // CHUNK, cols // PAIR
    order = lambda i: i
    tok = token_spec(cols, order)
    sq = square_spec(pairs, order)
    sq_shape = jax.ShapeDtypeStruct((steps, pairs, PAIR, PAIR), F32)
    tok_shape = jax.ShapeDtypeStruct((tokens, cols), F32)
    return pl.pallas_call(
        forward_kernel,
        name="mixer_forward",
        grid=(steps,),
        in_specs=mixer_specs(cols, order),
        out_specs=[tok, tok, tok] + [sq] * 5,
        out_shape=[jax.ShapeDtypeStruct((tokens, cols), BF), tok_shape, tok_shape] + [sq_shape] * 5,
        scratch_shapes=[pltpu.VMEM((pairs, PAIR, PAIR), F32)],
        compiler_params=pltpu.CompilerParams(vmem_limit_bytes=48 << 20),
        cost_estimate=pl.CostEstimate(
            flops=steps * pairs * 600 * PAIR**3,
            bytes_accessed=22 << 20,
            transcendentals=8 * tokens * cols,
        ),
    )(r, *rest)


def mixer_backward(dz, r, *rest):
    tokens, cols = r.shape
    steps, pairs = tokens // CHUNK, cols // PAIR
    order = lambda i: steps - 1 - i
    tok = token_spec(cols, order)
    wide = token_spec(4 * cols, order)
    sq = square_spec(pairs, order)
    low = jax.ShapeDtypeStruct((tokens, cols), BF)
    return pl.pallas_call(
        backward_kernel,
        name="mixer_backward",
        grid=(steps,),
        in_specs=[tok] + mixer_specs(cols, order) + [tok, tok] + [sq] * 5,
        out_specs=[tok, tok, tok, wide, tok, pl.BlockSpec((8, cols), lambda i: (0, 0))],
        out_shape=[low] * 3
        + [
            jax.ShapeDtypeStruct((tokens, 4 * cols), BF),
            jax.ShapeDtypeStruct((tokens, cols), F32),
            jax.ShapeDtypeStruct((8, cols), F32),
        ],
        scratch_shapes=[pltpu.VMEM((pairs, PAIR, PAIR), F32)],
        compiler_params=pltpu.CompilerParams(vmem_limit_bytes=48 << 20),
        cost_estimate=pl.CostEstimate(
            flops=steps * pairs * 600 * PAIR**3,
            bytes_accessed=28 << 20,
            transcendentals=8 * tokens * cols,
        ),
    )(dz, r, *rest)


def part_masks(parts, total):
    lane = lax.broadcasted_iota(jnp.int32, (1, total), 1)
    return [((lane >= a) & (lane < b)).astype(F32).astype(BF) for a, b in parts]


def halves(value, own, rows):
    value = value.reshape(-1, 2, rows, value.shape[-1])
    flag = own == 1
    sent = jnp.where(flag, value[:, 0], value[:, 1])
    kept = jnp.where(flag, value[:, 1], value[:, 0])
    shape = (-1, value.shape[-1])
    return sent.reshape(shape).astype(BF), kept.reshape(shape).astype(BF)


def weight_grad_kernel(rows, sizes, own_ref, *refs):
    count = sum(sizes)
    left, right = refs[:count], refs[count : 2 * count]
    outs = refs[2 * count :]
    at = 0
    for i, size in enumerate(sizes):
        for k in range(size):
            value = lax.dot_general(left[at][...], right[at][...], TN, preferred_element_type=F32)
            sent, kept = halves(value, own_ref[0], rows)
            outs[2 * i][k] = sent
            outs[2 * i + 1][k] = kept
            at += 1


def weight_grads(own, rows, sizes, left, right):
    tokens, width = left[0].shape
    block = column_block(width)
    count = len(left)
    out_specs, out_shape, at = [], [], 0
    for size in sizes:
        cols = right[at].shape[1]
        at += size
        out_specs += [pl.BlockSpec((size, block // 2, cols), lambda j, own: (0, j, 0))] * 2
        out_shape += [jax.ShapeDtypeStruct((size, width // 2, cols), BF)] * 2
    out = pl.pallas_call(
        lambda *refs: weight_grad_kernel(rows, sizes, *refs),
        name="weight_grads",
        grid_spec=pltpu.PrefetchScalarGridSpec(
            num_scalar_prefetch=1,
            grid=(width // block,),
            in_specs=[pl.BlockSpec((tokens, block), lambda j, own: (0, j))] * count
            + [pl.BlockSpec((tokens, r.shape[1]), lambda j, own: (0, 0)) for r in right],
            out_specs=out_specs,
        ),
        out_shape=out_shape,
        compiler_params=pltpu.CompilerParams(vmem_limit_bytes=56 << 20),
        cost_estimate=pl.CostEstimate(
            flops=2 * tokens * width * sum(r.shape[1] for r in right),
            bytes_accessed=12 << 20,
            transcendentals=0,
        ),
    )(own, *left, *right)
    return [(out[2 * i], out[2 * i + 1]) for i in range(len(sizes))]


def channel_grad_kernel(key_left, key_right, value_left, value_right, out_ref):
    for i, (left, right) in enumerate(((key_left, key_right), (value_left, value_right))):
        out_ref[i] = lax.dot_general(
            left[...], right[...], TN, preferred_element_type=F32
        ).astype(BF)


def channel_grads(channel_in, pre_grad, seed, hidden):
    tokens, width = channel_in.shape
    units = hidden.shape[1]
    block = column_block(width)
    rows = pl.BlockSpec((tokens, block), lambda j: (0, j))
    full = pl.BlockSpec((tokens, units), lambda j: (0, 0))
    return pl.pallas_call(
        channel_grad_kernel,
        name="channel_grads",
        grid=(width // block,),
        in_specs=[rows, full, rows, full],
        out_specs=pl.BlockSpec((2, block, units), lambda j: (0, j, 0)),
        out_shape=jax.ShapeDtypeStruct((2, width, units), BF),
        compiler_params=pltpu.CompilerParams(vmem_limit_bytes=56 << 20),
        cost_estimate=pl.CostEstimate(
            flops=4 * tokens * width * units, bytes_accessed=14 << 20, transcendentals=0
        ),
    )(channel_in, pre_grad, seed, hidden)


def column_block(total):
    return 256 if total % 256 == 0 else 128


def input_grad_kernel(
    parts, x_ref, mean_ref, scale_ref, keep_ref, gain_ref, bias_ref, lerp_ref,
    gr_ref, gk_ref, gv_ref, wr_ref, wk_ref, wv_ref, hidden_ref, first_ref, spread_ref, sums_ref,
):
    tokens = x_ref.shape[0]
    unit = (x_ref[...].astype(F32) - mean_ref[...]) * scale_ref[...]
    normed = (unit * gain_ref[...] + bias_ref[...]).astype(BF).astype(F32)
    keep = keep_ref[...]
    delta = pltpu.roll(normed, 1, 0) * keep - normed
    hidden = hidden_ref[...]
    masks = part_masks(parts, hidden.shape[1])
    low = [
        lax.dot_general(hidden * masks[i], first_ref[...], NT, preferred_element_type=F32)
        for i in range(4)
    ]

    def back(g_ref, w_ref):
        return lax.dot_general(g_ref[...], w_ref[...], NT, preferred_element_type=F32)

    grads = [
        back(gr_ref, wr_ref), low[0], back(gk_ref, wk_ref), back(gv_ref, wv_ref) + low[2], low[1], low[3],
    ]
    total = grads[0]
    carried = grads[0] * lerp_ref[0:1]
    for i in range(1, 6):
        total = total + grads[i]
        carried = carried + grads[i] * lerp_ref[i : i + 1]
    spread_rows = total - carried + pltpu.roll(carried * keep, tokens - 1, 0)
    spread_ref[...] = spread_rows
    rows = [jnp.sum(g * delta, 0, keepdims=True) for g in grads]
    rows.append(jnp.sum(spread_rows * unit, 0, keepdims=True))
    rows.append(jnp.sum(spread_rows, 0, keepdims=True))
    sums_ref[...] = jnp.concatenate(rows, 0)


def input_grads(x, mean, scale, keep, gain, bias, lerps, grads, weights, hidden, first, parts):
    tokens, width = x.shape
    cols = grads[0].shape[1]
    ranks = hidden.shape[1]
    block = column_block(width)
    side = lambda n: pl.BlockSpec((tokens, n), lambda j: (0, 0))
    top = lambda n: pl.BlockSpec((n, block), lambda j: (0, j))
    wide = lambda n: pl.BlockSpec((block, n), lambda j: (j, 0))
    return pl.pallas_call(
        lambda *refs: input_grad_kernel(parts, *refs),
        name="input_grads",
        grid=(width // block,),
        in_specs=[top(tokens), side(1), side(1), side(1), top(1), top(1), top(6)]
        + [side(cols)] * 3
        + [wide(cols)] * 3
        + [side(ranks), wide(ranks)],
        out_specs=[top(tokens), top(8)],
        out_shape=[jax.ShapeDtypeStruct((tokens, width), F32), jax.ShapeDtypeStruct((8, width), F32)],
        compiler_params=pltpu.CompilerParams(vmem_limit_bytes=48 << 20),
        cost_estimate=pl.CostEstimate(
            flops=8 * tokens * width * cols, bytes_accessed=10 << 20, transcendentals=0
        ),
    )(x, mean, scale, keep, gain, bias, lerps, *grads, *weights, hidden, first)


def lowrank_grad_kernel(
    parts, groups, place_ref, m1_ref, m4_ref, m3_ref, m5_ref, hidden_ref,
    g0_ref, g1_ref, g2_ref, g3_ref, inner_ref, par_ref,
    first_down_ref, first_up_ref, second_down_ref, second_up_ref, out_ref,
):
    hidden, inner = hidden_ref[...], inner_ref[...]
    ranks = hidden.shape[1]
    masks = part_masks(parts, ranks)
    total = out_ref.shape[-1]

    def turned(ref, start, step):
        count = ref.shape[0]
        spots = lax.broadcasted_iota(jnp.int32, (count, total), 1)
        row = lax.broadcasted_iota(jnp.int32, (count, total), 0)
        place = (spots == start + (row // 8) * step + row % 8).astype(F32).astype(BF)
        return mm(split(ref[...]), (place,), TN)

    def chain(refs, right):
        out = None
        for i, ref in enumerate(refs):
            term = lax.dot_general(ref[...], right * masks[i], TN, preferred_element_type=F32)
            out = term if out is None else out + term
        return jnp.pad(out, ((0, 0), (0, total - ranks)))

    down = chain((m1_ref, m4_ref, m3_ref, m5_ref), hidden)
    up = chain((g0_ref, g1_ref, g2_ref, g3_ref), inner)
    down = down + turned(first_down_ref, ranks, 16) + turned(second_down_ref, ranks + 8, 16)
    up = up + turned(first_up_ref, ranks, 16) + turned(second_up_ref, ranks + 8, 16)
    out_ref[0] = down
    out_ref[1] = up + turned(par_ref, ranks + 16 * groups, 0)


def lowrank_grads(place, mixed, hidden, low_grads, inner, par_grad, first, second, parts):
    tokens, width = mixed[0].shape
    cols = low_grads.shape[1] // 4
    ranks = hidden.shape[1]
    block = column_block(cols)
    steps = cols // block
    groups = first.shape[0] // 8
    total = ranks + 16 * groups + 8
    side = lambda n: pl.BlockSpec((tokens, n), lambda j, at: (0, 0))
    held = [pl.BlockSpec((tokens, block), lambda j, at: (0, at[0] * steps + j))] * 4
    low = [pl.BlockSpec((tokens, block), lambda j, at, i=i: (0, i * steps + j)) for i in range(4)]
    down = pl.BlockSpec((8 * groups, block), lambda j, at: (0, j))
    up = pl.BlockSpec((8 * groups, block), lambda j, at: (0, steps + j))
    return pl.pallas_call(
        lambda *refs: lowrank_grad_kernel(parts, groups, *refs),
        name="lowrank_grads",
        grid_spec=pltpu.PrefetchScalarGridSpec(
            num_scalar_prefetch=1,
            grid=(steps,),
            in_specs=held
            + [side(ranks)]
            + low
            + [side(ranks), pl.BlockSpec((8, block), lambda j, at: (0, j)), down, up, down, up],
            out_specs=pl.BlockSpec((2, block, total), lambda j, at: (0, j, 0)),
        ),
        out_shape=jax.ShapeDtypeStruct((2, cols, total), F32),
        compiler_params=pltpu.CompilerParams(vmem_limit_bytes=48 << 20),
        cost_estimate=pl.CostEstimate(
            flops=16 * tokens * cols * ranks, bytes_accessed=5 << 20, transcendentals=0
        ),
    )(place, *mixed, hidden, *([low_grads] * 4), inner, par_grad, first, first, second, second)


def unpack_kernel(ranks, extra, given_ref, down_ref, up_ref, par_ref, totals_ref):
    rows = given_ref[:, 0].astype(F32)
    rows = rows.reshape(-1, rows.shape[-1])
    heads = rows.shape[0] // 2
    down_ref[...] = rows[:heads, :ranks]
    turned = rows.T
    up_ref[...] = turned[:ranks, heads:]
    par_ref[...] = turned[ranks + extra :, heads:]

    @pl.when(pl.program_id(0) == 0)
    def _():
        totals_ref[...] = jnp.zeros_like(totals_ref)

    totals_ref[...] += turned[ranks : ranks + extra]


def unpack(given, ranks, extra):
    size, peers, rows, total = given.shape
    heads = size * rows // 2
    width = peers * heads
    return pl.pallas_call(
        lambda *refs: unpack_kernel(ranks, extra, *refs),
        name="unpack",
        grid=(peers,),
        in_specs=[pl.BlockSpec((size, 1, rows, total), lambda p: (0, p, 0, 0))],
        out_specs=[
            pl.BlockSpec((heads, ranks), lambda p: (p, 0)),
            pl.BlockSpec((ranks, heads), lambda p: (0, p)),
            pl.BlockSpec((8, heads), lambda p: (0, p)),
            pl.BlockSpec((extra, 2 * heads), lambda p: (0, 0)),
        ],
        out_shape=[
            jax.ShapeDtypeStruct((width, ranks), F32),
            jax.ShapeDtypeStruct((ranks, width), F32),
            jax.ShapeDtypeStruct((8, width), F32),
            jax.ShapeDtypeStruct((extra, 2 * heads), F32),
        ],
        compiler_params=pltpu.CompilerParams(vmem_limit_bytes=48 << 20),
    )(given)


def halving_kernel(has_other, own_ref, *refs):
    count = len(has_other)
    given = iter(refs[: count + sum(has_other)])
    results = refs[count + sum(has_other) :]
    for i in range(count):
        held_ref = next(given)
        other_ref = next(given) if has_other[i] else None
        mine = own_ref[i]

        def half(at):
            rows = held_ref[:, at].astype(F32)
            return rows if other_ref is None else rows + other_ref[:, at].astype(F32)

        results[2 * i][...] = half(1 - mine).astype(BF)
        results[2 * i + 1][...] = half(mine).astype(BF)


def halving(own, pieces):
    steps = 4 if all(held.shape[-1] % 512 == 0 for held, _ in pieces) else 1
    operands, in_specs, out_specs, out_shape = [], [], [], []
    for held, other in pieces:
        before, _, rows, cols = held.shape
        block = cols // steps
        for x in (held, other):
            if x is not None:
                operands.append(x)
                in_specs.append(pl.BlockSpec((before, 2, rows, block), lambda j, own: (0, 0, 0, j)))
        for dtype in (BF, BF):
            out_specs.append(pl.BlockSpec((before, rows, block), lambda j, own: (0, 0, j)))
            out_shape.append(jax.ShapeDtypeStruct((before, rows, cols), dtype))
    flags = [other is not None for _, other in pieces]
    total = sum(x.size for x in operands)
    results = pl.pallas_call(
        lambda *refs: halving_kernel(flags, *refs),
        name="halving",
        grid_spec=pltpu.PrefetchScalarGridSpec(
            num_scalar_prefetch=1, grid=(steps,), in_specs=in_specs, out_specs=out_specs
        ),
        out_shape=out_shape,
        compiler_params=pltpu.CompilerParams(vmem_limit_bytes=48 << 20),
        cost_estimate=pl.CostEstimate(flops=2 * total, bytes_accessed=6 * total, transcendentals=0),
    )(own, *operands)
    return [(results[2 * i], results[2 * i + 1]) for i in range(len(pieces))]


def document_tables(segments):
    rows, length = segments.shape
    marks = segments + (length + 1) * lax.broadcasted_iota(jnp.int32, (rows, length), 0)
    flat = marks.reshape(-1).astype(F32)
    blocks = flat.reshape(-1, CHUNK)
    ends = blocks[:, -1]
    before = jnp.concatenate([jnp.full((1,), -1.0, F32), ends[:-1]])
    wide = lambda x: jnp.broadcast_to(x[:, None], (x.shape[0], PAIR))
    aux = jnp.stack([jnp.concatenate([blocks, blocks], 1), wide(ends), wide(before)] + [jnp.zeros((blocks.shape[0], PAIR), F32)] * 5, 1)
    return flat[:, None], aux


def bit_positions(size):
    return [1 << i for i in reversed(range(size.bit_length() - 1))]


def swap(x, axis, bit):
    size = lax.axis_size(axis)
    return lax.ppermute(x, axis, [(i, i ^ bit) for i in range(size)])


def power_of_two(size):
    return size & (size - 1) == 0


def gather_rows(shard, axis, order=None):
    size = lax.axis_size(axis)
    if not power_of_two(size):
        return lax.all_gather(shard, axis, axis=0, tiled=True)
    place = lax.axis_index(axis)
    bits = bit_positions(size)
    held = shard.reshape((1,) * len(bits) + shard.shape)
    for bit in order or bits:
        spot = bits.index(bit)
        other = swap(held, axis, bit)
        held = jnp.where(
            (place & bit) != 0,
            jnp.concatenate([other, held], spot),
            jnp.concatenate([held, other], spot),
        )
    return held.reshape((size * shard.shape[0],) + shard.shape[1:])


class Piece:
    def __init__(self, full, dim, axis, side_last=False):
        bits = bit_positions(lax.axis_size(axis))
        self.order = bits[::-1]
        if side_last:
            self.order = bits[-1:] + bits[:-2][::-1] + bits[-2:-1]
        self.lead, self.rows = full.shape[:dim], full.shape[dim] // lax.axis_size(axis)
        self.cols = full.shape[-1]
        self.held, self.other, self.left, self.axis = full, None, bits, axis

    def view(self, x, bit):
        spot = self.left.index(bit)
        before = 1
        for n in self.lead + (2,) * spot:
            before *= n
        return None if x is None else x.reshape(before, 2, -1, self.cols)

    def move(self, sent, bit):
        self.other = swap(sent, self.axis, bit)
        self.left = [b for b in self.left if b != bit]

    def total(self):
        shape = self.lead + (self.rows, self.cols)
        return self.held.reshape(shape) + self.other.reshape(shape).astype(F32)


def begun(pair, rows, axis, side_last=False):
    sent, kept = pair
    piece = Piece(kept, 1, axis, side_last)
    piece.rows = rows
    piece.move(sent, piece.order.pop(0))
    return piece


def prepare(*pieces):
    pieces = [piece for piece in pieces if piece.order]
    if not pieces:
        return []
    bits = [piece.order.pop(0) for piece in pieces]
    held = [(p.view(p.held, bit), p.view(p.other, bit)) for p, bit in zip(pieces, bits)]
    own = jnp.stack([((lax.axis_index(p.axis) & bit) != 0).astype(jnp.int32) for p, bit in zip(pieces, bits)])
    moves = []
    for piece, bit, (sent, kept) in zip(pieces, bits, halving(own, held)):
        piece.held = kept
        moves.append((piece, sent, bit))
    return moves


def launch(moves):
    for piece, sent, bit in moves:
        piece.move(sent, bit)


def advance(*pieces):
    launch(prepare(*pieces))


def join_peers(partial, sent, axis):
    size = lax.axis_size(axis)
    if size != 2:
        return lax.psum(partial, axis)
    return partial + swap(sent, axis, 1).astype(F32)


def add_peers(partial, axis):
    return join_peers(partial, partial.astype(BF), axis)


def scatter_peers(partial, axis):
    size = lax.axis_size(axis)
    if size != 2:
        return lax.psum_scatter(partial, axis, scatter_dimension=0, tiled=True)
    rows = partial.shape[0] // 2
    place = lax.axis_index(axis)
    sent = lax.dynamic_slice_in_dim(partial, (1 - place) * rows, rows, 0).astype(BF)
    kept = lax.dynamic_slice_in_dim(partial, place * rows, rows, 0)
    return kept + swap(sent, axis, 1).astype(F32)


def rounded(x):
    return lax.reduce_precision(x, 8, 7)


def normalized(rows):
    mean = jnp.mean(rows, -1, keepdims=True)
    centred = rows - mean
    scale = lax.rsqrt(jnp.mean(centred * centred, -1, keepdims=True) + 1e-05)
    return centred * scale, mean, scale


def norm_back(grad, unit, scale, gain):
    inner = grad * gain
    return scale * (
        inner
        - jnp.mean(inner, -1, keepdims=True)
        - unit * jnp.mean(inner * unit, -1, keepdims=True)
    )


def on_device(
    block_input,
    first_layer_values,
    segments,
    valid,
    cotangent,
    teacher,
    layer_norm_gain,
    layer_norm_bias,
    lerps,
    decay_offset,
    head_gain_table,
    per_unit_shift_array,
    lowrank_first_maps,
    lowrank_second_maps,
    receptance_key_value_weight,
    time_output_weight,
    channel_key_weight,
    channel_value_weight,
):
    tensor_size = lax.axis_size("tensor")
    tensor_pos = lax.axis_index("tensor")
    dp_pos = lax.axis_index("dp")
    own_rows, width = block_input.shape
    tokens = own_rows * tensor_size
    heads = receptance_key_value_weight.shape[2]
    units = channel_key_weight.shape[1]
    column_begin = tensor_pos * heads
    row_begin = tensor_pos * own_rows
    cut_one, cut_two = DECAY_MAP_RANK, DECAY_MAP_RANK + RATE_MAP_RANK
    cut_three = cut_two + VALUE_MIX_RANK
    ranks = lowrank_first_maps.shape[1]
    parts = ((0, DECAY_MAP_RANK), (DECAY_MAP_RANK, cut_two), (cut_two, cut_three), (cut_three, ranks))

    dp_own = (dp_pos & 1)[None].astype(jnp.int32)
    dp_rows = width // lax.axis_size("dp")
    block_low = gather_rows(block_input, "tensor")
    mixer_full = lax.all_gather(
        jnp.concatenate([w for w in receptance_key_value_weight] + [time_output_weight.T], 1),
        "dp",
        axis=0,
        tiled=True,
    )
    wide_full = lax.all_gather(
        jnp.concatenate([channel_key_weight, channel_value_weight.T], 1), "dp", axis=0, tiled=True
    )
    key_full, value_full = wide_full[:, :units], wide_full[:, units:]
    rkv_full = [mixer_full[:, i * heads : (i + 1) * heads] for i in range(3)]
    out_full = mixer_full[:, 3 * heads :]
    block_rows = block_low.astype(F32)
    teacher, cotangent, block_low = lax.optimization_barrier((teacher, cotangent, block_low))
    teacher_low = gather_rows(teacher, "tensor")
    cotangent_low = gather_rows(cotangent, "tensor")
    valid_all = valid.astype(F32).reshape(-1)
    valid_count = jnp.sum(valid_all)
    valid_rows = lax.dynamic_slice_in_dim(valid_all, dp_pos * tokens, tokens)[:, None]
    same_doc = (segments[:, 1:] == segments[:, :-1]).astype(F32)
    retain_mask = jnp.concatenate([jnp.zeros((segments.shape[0], 1), F32), same_doc], 1).reshape(-1)
    row_index = lax.broadcasted_iota(jnp.int32, (tokens, 1), 0)
    own_mask = ((row_index >= row_begin) & (row_index < row_begin + own_rows)).astype(F32)

    unit_one, mean_one, scale_one = normalized(block_rows)
    normed_one = rounded(unit_one * layer_norm_gain[0] + layer_norm_bias[0])
    delta_one = shift_down(normed_one, retain_mask) - normed_one
    blended = [(normed_one + delta_one * lerps[i]).astype(BF) for i in range(6)]
    receptance = matrix_multiply(blended[0], rkv_full[0])
    key_rows = matrix_multiply(blended[2], rkv_full[1])
    value_rows = matrix_multiply(blended[3], rkv_full[2])
    lane = lax.broadcasted_iota(jnp.int32, (1, ranks), 1)
    lanes = (1, 4, 3, 5)
    before = sum(
        matrix_multiply(
            blended[lanes[i]],
            jnp.where((lane >= parts[i][0]) & (lane < parts[i][1]), lowrank_first_maps, 0),
        )
        for i in range(4)
    )
    squashed = jnp.tanh(before)
    gated = jax.nn.sigmoid(before)
    is_decay, is_gate = lane < cut_one, lane >= cut_three
    inner = jnp.where(is_decay, squashed, jnp.where(is_gate, gated, before)).astype(BF)
    slope = jnp.where(is_decay, 1.0 - squashed * squashed, jnp.where(is_gate, gated * (1.0 - gated), 1.0))
    upper = lax.dynamic_slice_in_dim(lowrank_second_maps, column_begin, heads, 1)
    rank_row = lax.broadcasted_iota(jnp.int32, (ranks, 1), 0)
    upper_wide = jnp.concatenate(
        [jnp.where((rank_row >= a) & (rank_row < b), upper, 0) for a, b in parts], 1
    )
    low_rows = matrix_multiply(inner, upper_wide)
    par = lax.dynamic_slice_in_dim(
        jnp.concatenate([decay_offset[None], head_gain_table, per_unit_shift_array], 0),
        column_begin,
        heads,
        1,
    )
    doc_col, doc_aux = document_tables(segments)
    mixer_args = (
        receptance, key_rows, value_rows, low_rows, first_layer_values, par, doc_col, doc_aux,
    )
    mixed, *kept = mixer_forward(*mixer_args)
    mixed, teacher_low, cotangent_low = lax.optimization_barrier((mixed, teacher_low, cotangent_low))
    after_mixer = block_rows + add_peers(matrix_multiply_transposed(mixed, out_full), "tensor")
    unit_two, _, scale_two = normalized(after_mixer)
    normed_two = rounded(unit_two * layer_norm_gain[1] + layer_norm_bias[1])
    delta_two = shift_down(normed_two, retain_mask) - normed_two
    channel_in = (normed_two + delta_two * lerps[6]).astype(BF)
    rectified = jnp.maximum(matrix_multiply(channel_in, key_full), 0.0)
    hidden = (rectified * rectified).astype(BF)
    block_sum = after_mixer + add_peers(matrix_multiply_transposed(hidden, value_full), "tensor")
    block_out = lax.dynamic_slice_in_dim(block_sum, row_begin, own_rows, 0).astype(BF)
    mismatch = block_sum - teacher_low.astype(F32)
    norm = valid_count * width
    loss_part = jnp.sum(valid_rows * own_mask * mismatch * mismatch) / norm
    loss_row = jnp.full((1, width), loss_part, F32)
    seed = valid_rows * (cotangent_low.astype(F32) + 2.0 * mismatch / norm)
    seed_low = seed.astype(BF)
    pre_grad = (matrix_multiply(seed_low, value_full) * 2.0 * rectified).astype(BF)
    channel_back = matrix_multiply_transposed(pre_grad, key_full)
    lerp_six = jnp.sum(channel_back * delta_two, 0)
    spread_two = channel_back * (1.0 - lerps[6]) + shift_up(channel_back * lerps[6], retain_mask)
    gain_two = jnp.sum(spread_two * unit_two, 0)
    bias_two = jnp.sum(spread_two, 0)
    early = jnp.concatenate(
        [gain_two[None], bias_two[None], lerp_six[None], loss_row, jnp.zeros((4, width), F32)], 0
    )
    normed_two_sent = spread_two.astype(BF)
    normed_two_sent, pre_grad, seed_low = lax.optimization_barrier((normed_two_sent, pre_grad, seed_low))
    normed_two_grad = join_peers(spread_two, normed_two_sent, "tensor")
    channel_part = channel_grads(channel_in, pre_grad, seed_low, hidden)
    channel_grad = lax.psum_scatter(channel_part, "dp", scatter_dimension=1, tiled=True)
    after_grad = seed + norm_back(normed_two_grad, unit_two, scale_two, layer_norm_gain[1])
    after_low = after_grad.astype(BF)
    mixer_grad = matrix_multiply(after_low, out_full)
    recept_low, key_low, value_low, low_grads, first_grad, par_grad = mixer_backward(
        mixer_grad, *mixer_args, *kept
    )
    hidden_part = matrix_multiply_transposed(low_grads, upper_wide) * slope
    hidden_sent = hidden_part.astype(BF)
    hidden_sent, recept_low, key_low, value_low = lax.optimization_barrier(
        (hidden_sent, recept_low, key_low, value_low)
    )
    hidden_grad = join_peers(hidden_part, hidden_sent, "tensor").astype(BF)
    first_halves, second_halves = weight_grads(
        dp_own,
        dp_rows,
        (2, 2),
        [blended[0], blended[2], blended[3], after_low],
        [recept_low, key_low, value_low, mixed],
    )
    first = begun(first_halves, dp_rows, "dp")
    second = begun(second_halves, dp_rows, "dp", True)
    hidden_grad, first.other, second.other = lax.optimization_barrier(
        (hidden_grad, first.other, second.other)
    )
    advance(first, second)
    spread_one, sums = input_grads(
        block_low,
        mean_one,
        scale_one,
        retain_mask[:, None],
        layer_norm_gain[:1],
        layer_norm_bias[:1],
        lerps[:6],
        [recept_low, key_low, value_low],
        rkv_full,
        hidden_grad * own_mask.astype(BF),
        lowrank_first_maps,
        parts,
    )
    normed_one_grad = scatter_peers(spread_one, "tensor")
    groups = width // (2 * heads)

    def folded(x):
        return jnp.moveaxis(x.reshape(8, groups, 2 * heads), 1, 0).reshape(8 * groups, 2 * heads)

    low_part = lowrank_grads(
        tensor_pos[None].astype(jnp.int32),
        [blended[i] for i in lanes],
        hidden_grad,
        low_grads,
        inner,
        par_grad,
        folded(sums),
        folded(early),
        parts,
    )
    low_part, channel_grad = lax.optimization_barrier((low_part, channel_grad))
    low_piece = Piece(low_part.reshape(2 * heads, -1), 0, "dp")
    while low_piece.order:
        advance(low_piece)
        advance(first, second)
    while first.order or second.order:
        advance(first, second)
    grad_key, grad_value = channel_grad[0].astype(F32), channel_grad[1].astype(F32).T
    first_grads, second_grads = first.total(), second.total()
    grad_rkv = jnp.stack([first_grads[0], first_grads[1], second_grads[0]])
    grad_out = second_grads[1].T
    low_pair = gather_rows(low_piece.total().astype(BF)[None], "tensor")
    grad_down, grad_up, par_total, totals = unpack(gather_rows(low_pair[None], "dp"), ranks, 16 * groups)
    totals = jnp.moveaxis(totals.reshape(groups, 16, 2 * heads), 0, 1).reshape(16, width)

    def own(x):
        return lax.dynamic_slice_in_dim(x, row_begin, own_rows, 0)

    grad_in = own(after_grad) + norm_back(normed_one_grad, own(unit_one), own(scale_one), layer_norm_gain[0])
    return (
        block_out,
        totals[11, 0],
        grad_in,
        first_grad,
        jnp.stack([totals[6], totals[8]]),
        jnp.stack([totals[7], totals[9]]),
        jnp.concatenate([totals[0:1], totals[2:6], totals[10:11]], 0),
        totals[1],
        par_total[0],
        par_total[1:4],
        par_total[4:8],
        grad_down,
        grad_up,
        grad_rkv,
        grad_out,
        grad_key,
        grad_value,
    )


def solution(mesh):
    return jax.shard_map(
        on_device,
        mesh=mesh,
        in_specs=(
            P(("dp", "tensor"), None),
            P("dp", "tensor"),
            P("dp", None),
            P(),
            P(("dp", "tensor"), None),
            P(("dp", "tensor"), None),
            P(),
            P(),
            P(),
            P(),
            P(),
            P(),
            P(),
            P(),
            P(None, "dp", "tensor"),
            P("tensor", "dp"),
            P("dp", "tensor"),
            P("tensor", "dp"),
        ),
        out_specs=(
            P(("dp", "tensor"), None),
            P(),
            P(("dp", "tensor"), None),
            P("dp", "tensor"),
            P(),
            P(),
            P(),
            P(),
            P(),
            P(),
            P(),
            P(),
            P(),
            P(None, "dp", "tensor"),
            P("tensor", "dp"),
            P("dp", "tensor"),
            P("tensor", "dp"),
        ),
        check_vma=False,
    )
```

time: 1070 us -> 423 us (0.40)
  waiting for transfers between devices: 771 us -> 141 us
  Pallas kernels: 72 us -> 114 us
  blocking collectives: 41.6 us -> 0 us
  matrix products: 80 us -> 39.5 us
  starting transfers between devices: 1.37 us -> 26.9 us
    reduce_scatter x9 -> x1, waiting for transfers between devices: 469 us -> 0.01 us  [on_device(): lax.psum_scatter(channel_part, 'dp', scatter_dimension=1, tiled=True)]
    all_gather x8 -> x2, waiting for transfers between devices: 212 us -> 13.4 us  [the longest x1 9.63 us: on_device(): lax.all_gather(jnp.concatenate([w for w in receptance_key_value_weight] +...]
    ppermute x0 -> x25, waiting for transfers between devices: none -> 127 us  [swap(): return lax.ppermute(x, axis, [(i, i ^ bit) for i in range(size)])]
    psum x1 -> x0, waiting for transfers between devices: 88.2 us -> none  [on_device(): lax.psum((small_terms[0], small_terms[1], small_terms[2], small_terms[3],...]
    psum x1 -> x0, blocking collectives: 41.6 us -> none  [on_device(): lax.psum((small_terms[0], small_terms[1], small_terms[2], small_terms[3],...]
    pallas_call x0 -> x12, Pallas kernels: none -> 41.5 us  [the longest x1 9.14 us: channel_grads(): pl.pallas_call(channel_grad_kernel, name='channel_grads', grid=(width //...]
    ppermute x0 -> x25, starting transfers between devices: none -> 26.8 us  [swap(): return lax.ppermute(x, axis, [(i, i ^ bit) for i in range(size)])]
    dot_general x14 -> x0, matrix products: 24.7 us -> none  [matmul_tn(): lax.dot_general(left, right, (((0,), (0,)), ((), ())), preferred_element_...]
  transfers between devices with their start and end apart: 18 -> 28, of which waited for: 16 -> 15; matrix products, arithmetic and copies ran while one was open for 8% -> 17% of each run, Pallas kernels for 3% -> 25%
where the time goes in v1:
time: 423 us; the launch traced here: 419 us
  waiting for transfers between devices  141 us (33%)
  Pallas kernels  114 us (27%)
  other arithmetic  45.2 us (11%)
  matrix products  39.5 us (9%)
  local copies, waits for them, and re-layouts  36.2 us (9%)
  starting transfers between devices  26.9 us (6%)
  between operations  16.7 us (4%)
    ppermute x25, waiting for transfers between devices, swap(): return lax.ppermute(x, axis, [(i, i ^ bit) for i in range(size)])  127 us
    pallas_call x1, Pallas kernels, mixer_backward(): pl.pallas_call(backward_kernel, name='mixer_backward', grid=(steps,), in_...  38.2 us
    pallas_call x1, Pallas kernels, mixer_forward(): pl.pallas_call(forward_kernel, name='mixer_forward', grid=(steps,), in_sp...  34.2 us
    dot_general x11, matrix products, matrix_multiply(): return jnp.dot(left, right, preferred_element_type=jnp.float32)  27.7 us
    ppermute x25, starting transfers between devices, swap(): return lax.ppermute(x, axis, [(i, i ^ bit) for i in range(size)])  26.8 us
    unnamed x214, local copies, waits for them, and re-layouts  19.6 us
    dot_general x4, matrix products, matrix_multiply_transposed(): lax.dot_general(left, right, (((1,), (1,)), ((), ())), preferred_element_...  11.7 us
    all_gather x1, waiting for transfers between devices, on_device(): lax.all_gather(jnp.concatenate([w for w in receptance_key_value_weight] +...  9.63 us
  transfers between devices with their start and end apart: 28, of which 15 were waited for; matrix products, arithmetic and copies ran while one was open for 17% of the time, Pallas kernels for 25%

profile of v1, /device:TPU:0, one launch (start us, length us, event | category | flops | bytes accessed | tf_op | source)
XLA Modules:
  0.0 419.0 jit_solution(17921454141297383344)
XLA Ops:
  17.8 9.1 %collective-permute-done = bf16[1,256,1024]{2,1,0:T(8,128)(2,1)S(1)} collective-permute-done((bf16[1,256,1024]{2,1,0:T(8,128)(2,1)S(1)}, bf16[1,256,1024]{2,1,0:T(8,128)(2,1)S(1)}, u32[]{:S(2)}, u32[]{:S(2)}) %collective-permute-start) | collective-permute-done | bytes 524320 | tf_op jit(solution)/shard_map/ppermute | solution.py:806
  44.9 8.5 %collective-permute-done.2 = bf16[1,256,1024]{2,1,0:T(8,128)(2,1)S(1)} collective-permute-done((bf16[1,256,1024]{2,1,0:T(8,128)(2,1)S(1)}, bf16[1,256,1024]{2,1,0:T(8,128)(2,1)S(1)}, u32[]{:S(2)}, u32[]{:S(2)}) %collective-permute-start.2) | collective-permute-done | bytes 524320 | tf_op jit(solution)/shard_map/ppermute | solution.py:806
  54.5 9.6 %all-gather.3.cloned.1.call-done = bf16[1024,2048]{1,0:T(8,128)(2,1)} async-done(((bf16[64,2048]{1,0:T(8,128)(2,1)}), bf16[1024,2048]{1,0:T(8,128)(2,1)}) %all-gather.3.cloned.1.call-update) | async-done | bytes 4194320 | tf_op jit(solution)/shard_map/all_gather | solution.py:967
  71.0 34.2 %mixer_forward.1 = (bf16[512,512]{1,0:T(8,128)(2,1)S(1)}, f32[512,512]{1,0:T(8,128)S(1)}, f32[512,512]{1,0:T(8,128)S(1)}, f32[8,4,128,128]{3,2,1,0:T(8,128)}, f3...) custom-call(f32[512,512]{1,0:T(8,128)S(1)} %fusion.64.r_ref, ...), custom_call_target="tpu_custom_call" | custom-call | flops 40265318400 | bytes 23068672 | tf_op jit(solution)/shard_map/mixer_forward/pallas_call | solution.py:440
  108.2 23.8 %collective-permute-done.3 = bf16[512,1024]{1,0:T(8,128)(2,1)S(1)} collective-permute-done((bf16[512,1024]{1,0:T(8,128)(2,1)S(1)}, bf16[512,1024]{1,0:T(8,128)(2,1)S(1)}, u32[]{:S(2)}, u32[]{:S(2)}) %collective-permute-start.3) | collective-permute-done | bytes 1048608 | tf_op jit(solution)/shard_map/ppermute | solution.py:806
  140.3 7.0 %multiply_convert_fusion.1 = (bf16[512,2048]{1,0:T(8,128)(2,1)S(1)}, f32[512,2048]{1,0:T(8,128)}) fusion(bf16[512,1024]{1,0:T(8,128)(2,1)} %add_convert_fusion.key_left, bf16[1024,4096]{1,0:T(8,128)(2,1)} %all-gather.5.cloned.1.call-done), kind=kOutput, calls=%fused_computation.1 | convolution fusion | flops 2150629376 | bytes 11534336 | tf_op jit(solution)/shard_map/dot_general | solution.py:20
  154.4 22.7 %collective-permute-done.4 = bf16[512,1024]{1,0:T(8,128)(2,1)} collective-permute-done((bf16[512,1024]{1,0:T(8,128)(2,1)}, bf16[512,1024]{1,0:T(8,128)(2,1)}, u32[]{:S(2)}, u32[]{:S(2)}) %collective-permute-start.4) | collective-permute-done | bytes 1048608 | tf_op jit(solution)/shard_map/ppermute | solution.py:806
  177.1 4.5 %fusion.13 = (f32[]{:T(128)}, f32[512,1024]{1,0:T(8,128)S(1)}) fusion(bf16[512,1024]{1,0:T(8,128)(2,1)} %bitcast.179, f32[512]{0:T(512)S(1)} %get-tuple-element.183, f32[512,1024]{1,0:T(8,128)} %copy-done.40, f32[512,1024]{1,0:T(8,128)} %get-tuple-element.252, bf16[512,1024]{1,0:T(8,128)(2,1)} %collective-permute-done.4), kind=kLoop, calls=%fused_computation.18 | loop fusion | flops 4194303 | bytes 8390660 | tf_op jit(solution)/shard_map/reduce_sum | solution.py:1041
  183.8 4.7 %multiply_convert_fusion.key_right = bf16[512,2048]{1,0:T(8,128)(2,1)S(1)} fusion(f32[512,2048]{1,0:T(8,128)} %get-tuple-element.250, bf16[512,1024]{1,0:T(8,128)(2,1)S(1)} %fusion.66.value_left, bf16[1024,4096]{1,0:T(8,128)(2,1)S(1)} %copy-done.97), kind=kOutput, calls=%fused_computation | convolution fusion | flops 2151677952 | bytes 11534336 | tf_op jit(solution)/shard_map/dot_general | solution.py:20
  196.3 9.1 %channel_grads.1 = bf16[2,1024,2048]{2,1,0:T(8,128)(2,1)} custom-call(bf16[512,1024]{1,0:T(8,128)(2,1)} %add_convert_fusion.key_left, bf16[512,2048]{1,0:T(8,128)(2,1)} %copy-done.101, bf16[512,1024]{1,0:T(8,128)(2,1)} %copy-done.57, bf16[512,2048]{1,0:T(8,128)(2,1)} %copy-done.100), custom_call_target="tpu_custom_call" | custom-call | flops 4294967296 | bytes 14680064 | tf_op jit(solution)/shard_map/channel_grads/pallas_call | solution.py:559
  207.0 23.4 %collective-permute-done.5 = bf16[512,1024]{1,0:T(8,128)(2,1)} collective-permute-done((bf16[512,1024]{1,0:T(8,128)(2,1)}, bf16[512,1024]{1,0:T(8,128)(2,1)}, u32[]{:S(2)}, u32[]{:S(2)}) %collective-permute-start.5) | collective-permute-done | bytes 1048608 | tf_op jit(solution)/shard_map/ppermute | solution.py:806
  230.4 4.2 %multiply_reduce_fusion.1 = (f32[1024]{0:T(1024)}, f32[512]{0:T(512)S(1)}, f32[512]{0:T(512)S(1)}, f32[1024]{0:T(1024)}) fusion(f32[512,1024]{1,0:T(8,128)} %get-tuple-element.188, f32[512,1024]{1,0:T(8,128)} %copy-done.40, f32[512]{0:T(512)S(1)} %add_rsqrt_fusion, f32[512]{0:T(512)S(1)} %broadcast_multiply_fusion.3, f32[1024]{0:T(1024)S(1)} %bitcast.199, ...), kind=kLoop, calls=%fused_computation.22 | loop fusion | flops 5764096 | bytes 5263360 | tf_op jit(solution)/shard_map/reduce_sum | solution.py:1049
  234.6 4.7 %fusion.67 = (bf16[512,1024]{1,0:T(8,128)(2,1)S(1)}, f32[512,1024]{1,0:T(8,128)}) fusion(f32[512]{0:T(512)S(1)} %broadcast_multiply_fusion.1, f32[512,1024]{1,0:T(8,128)S(1)} %copy-done.42, f32[512]{0:T(512)S(1)} %broadcast_multiply_fusion.3, f32[512]{0:T(512)S(1)} %broadcast_multiply_fusion.2, f32[1024]{0:T(1024)S(1)} %bitcast.200, ...), kind=kLoop, calls=%fused_computation.177 | loop fusion | flops 9437184 | bytes 12597252 | tf_op jit(solution)/shard_map/convert_element_type | solution.py:1060
  241.8 38.2 %mixer_backward.1 = (bf16[512,512]{1,0:T(8,128)(2,1)S(1)}, bf16[512,512]{1,0:T(8,128)(2,1)S(1)}, bf16[512,512]{1,0:T(8,128)(2,1)S(1)}, bf16[512,2048]{1,0:T(8,12...) custom-call(f32[512,512]{1,0:T(8,128)S(1)} %fusion.15.dz_ref, f32[512,512]{1,0:T(8,128)S(1)} %copy-done.37, ...), custom_call_target="tpu_custom_call" | custom-call | flops 40265318400 | bytes 29360128 | tf_op jit(solution)/shard_map/mixer_backward/pallas_call | solution.py:465
  280.1 4.5 %fusion.76 = (bf16[512,288]{1,0:T(8,128)(2,1)}, f32[512,288]{1,0:T(8,128)}) fusion(f32[512,288]{1,0:T(8,128)S(1)} %copy-done.102, pred[288]{0:T(512)(128)(4,1)S(1)} %copy-done.99, pred[288]{0:T(512)(128)(4,1)S(1)} %copy-done.93, bf16[512,2048]{1,0:T(8,128)(2,1)} %get-tuple-element.93.refs_6_.refs_7_.refs_8_.refs_9_, bf16[288,512]{1,0:T(8,128)(2,1)S(1)} %copy-done.70, ...), kind=kOutput, calls=%fused_computation.186 | convolution fusion | flops 610320384 | bytes 4751936 | tf_op jit(solution)/shard_map/dot_general | solution.py:30
  284.7 7.3 %weight_grads.1 = (bf16[2,512,512]{2,1,0:T(8,128)(2,1)}, bf16[2,512,512]{2,1,0:T(8,128)(2,1)}, bf16[2,512,512]{2,1,0:T(8,128)(2,1)}, bf16[2,512,512]{2,1,0:T(8,128)(2,1)}) custom-call(s32[1]{0:T(128)} %bitcast.32.refs_0_, bf16[512,1024]{1,0:T(8,128)(2,1)} %get-tuple-element.201.refs_1_, bf16[512,1024]{1,0:T(8,128)(2,1)} %get-tuple-element.197.refs_2_, ...), custom_call_target="tpu_custom_call" | custom-call | flops 2147483648 | bytes 12582912 | tf_op jit(solution)/shard_map/weight_grads/pallas_call | solution.py:525
  303.1 6.3 %collective-permute-done.6 = bf16[512,288]{1,0:T(8,128)(2,1)S(1)} collective-permute-done((bf16[512,288]{1,0:T(8,128)(2,1)}, bf16[512,288]{1,0:T(8,128)(2,1)S(1)}, u32[]{:S(2)}, u32[]{:S(2)}) %collective-permute-start.6) | collective-permute-done | bytes 294944 | tf_op jit(solution)/shard_map/ppermute | solution.py:806
  309.6 4.6 %halving.11 = (bf16[8,64,512]{2,1,0:T(8,128)(2,1)}, bf16[8,64,512]{2,1,0:T(8,128)(2,1)S(1)}, bf16[4,128,512]{2,1,0:T(8,128)(2,1)}, bf16[4,128,512]{2,1,0:T(8,128)(2,1)S(1)}) custom-call(s32[2]{0:T(128)S(1)} %pad_add_fusion.3.refs_0_, bf16[8,2,64,512]{3,2,1,0:T(8,128)(2,1)S(1)} %bitcast.154, bf16[8,2,64,512]{3,2,1,0:T(8,128)(2,1)S(1)} %bitcast.156, ...), custom_call_target="tpu_custom_call" | custom-call | flops 4194304 | bytes 12582912 | tf_op jit(solution)/shard_map/halving/pallas_call | solution.py:775
  316.0 8.7 %input_grads.1 = (f32[512,1024]{1,0:T(8,128)}, f32[8,1024]{1,0:T(8,128)S(1)}) custom-call(bf16[512,1024]{1,0:T(8,128)(2,1)S(1)} %bitcast.151, f32[512,1]{1,0:T(8,128)S(1)} %bitcast.161, f32[512,1]{1,0:T(8,128)S(1)} %copy-done.19, f32[512,1]{1,0:T(8,128)S(1)} %copy-done.18, f32[1,1024]{1,0:T(1,128)S(1)} %get-tuple-element.237.refs_4_, ...), custom_call_target="tpu_custom_call" | custom-call | flops 2147483648 | bytes 10485760 | tf_op jit(solution)/shard_map/input_grads/pallas_call | solution.py:620
  336.6 6.1 %lowrank_grads.1 = f32[2,512,312]{2,1,0:T(8,128)} custom-call(s32[1]{0:T(128)} %bitcast.30.refs_0_, bf16[512,1024]{1,0:T(8,128)(2,1)S(1)} %copy-done.6, bf16[512,1024]{1,0:T(8,128)(2,1)S(1)} %get-tuple-element.200.refs_2_, bf16[512,1024]{1,0:T(8,128)(2,1)S(1)} %copy-done.1, bf16[512,1024]{1,0:T(8,128)(2,1)S(1)} %copy-done.4, ...), custom_call_target="tpu_custom_call" | custom-call | flops 1207959552 | bytes 5242880 | tf_op jit(solution)/shard_map/lowrank_grads/pallas_call | solution.py:682
  359.9 6.1 %collective-permute-done.11 = bf16[2,64,312]{2,1,0:T(8,128)(2,1)S(1)} collective-permute-done((bf16[2,64,312]{2,1,0:T(8,128)(2,1)S(1)}, bf16[2,64,312]{2,1,0:T(8,128)(2,1)S(1)}, u32[]{:S(2)}, u32[]{:S(2)}) %collective-permute-start.11) | collective-permute-done | bytes 79904 | tf_op jit(solution)/shard_map/ppermute | solution.py:806
  379.1 7.0 %collective-permute-done.14 = bf16[1,1,1,1,1,2,64,312]{7,6,5,4,3,2,1,0:T(8,128)(2,1)S(1)} collective-permute-done((bf16[1,1,1,1,1,2,64,312]{7,6,5,4,3,2,1,0:T(8,128)(2,1)S(1)}, bf16[1,1,1,1,1,2,64,312]{7,6,5,4,3,2,1,0:T(8,128)(2,1)S(1)}, u32[]{:S(2)}, u32[]{:S(2)}) %collective-permute-start.14) | collective-permute-done | bytes 79904 | tf_op jit(solution)/shard_map/ppermute | solution.py:806
  386.4 5.5 %collective-permute-done.15 = bf16[2,1,1,1,1,2,64,312]{7,6,5,0,1,4,3,2:T(8,128)(2,1)S(1)} collective-permute-done((bf16[2,1,1,1,1,2,64,312]{7,6,5,0,1,4,3,2:T(8,128)(2,1)S(1)}, bf16[2,1,1,1,1,2,64,312]{7,6,5,0,1,4,3,2:T(8,128)(2,1)S(1)}, u32[]{:S(2)}, u32[]{:S(2)}) %collective-permute-start.15) | collective-permute-done | bytes 159776 | tf_op jit(solution)/shard_map/ppermute | solution.py:806
  394.2 6.6 %collective-permute-done.16 = bf16[2,2,1,1,1,2,64,312]{7,6,5,0,1,4,3,2:T(8,128)(2,1)S(1)} collective-permute-done((bf16[2,2,1,1,1,2,64,312]{7,6,5,0,1,4,3,2:T(8,128)(2,1)S(1)}, bf16[2,2,1,1,1,2,64,312]{7,6,5,0,1,4,3,2:T(8,128)(2,1)S(1)}, u32[]{:S(2)}, u32[]{:S(2)}) %collective-permute-start.16) | collective-permute-done | bytes 319520 | tf_op jit(solution)/shard_map/ppermute | solution.py:806
  (373 shorter events, 135.8 us)
Async XLA Ops:
  7.3 56.9 %all-gather.3.cloned.1.call-start = ((), (), s32[]{:S(2)}) async-start(), calls=%async_computation.1 | async-start | bytes 4456448 | tf_op jit(solution)/shard_map/all_gather | solution.py:967
  10.0 130.3 %all-gather.5.cloned.1.call-start = ((), (), s32[]{:S(2)}) async-start(), calls=%async_computation.2 | async-start | bytes 8912896 | tf_op jit(solution)/shard_map/all_gather | solution.py:973
  11.9 330.8 %reduce-scatter.2.cloned.1.call-start = ((), (), s32[]{:S(2)}) async-start(), calls=%async_computation.3 | async-start | bytes 8912896 | tf_op jit(solution)/shard_map/reduce_scatter | solution.py:1058
  12.0 15.0 %collective-permute-start = (bf16[1,256,1024]{2,1,0:T(8,128)(2,1)S(1)}, bf16[1,256,1024]{2,1,0:T(8,128)(2,1)S(1)}, u32[]{:S(2)}, u32[]{:S(2)}) collective-permute-start(bf16[1,256,1024]{2,1,0:T(8,128)(2,1)S(1)} %bitcast.190), channel_id=1, source_target_pairs={{0,1},{1,0},{2,3},{3,2},{4,5},{5,4},{6,7},{7,6},{8,9},{9,8},{10,11... | collective-permute-start | bytes 1572872 | tf_op jit(solution)/shard_map/ppermute | solution.py:806
  28.9 14.9 %collective-permute-start.1 = (bf16[1,256,1024]{2,1,0:T(8,128)(2,1)S(1)}, bf16[1,256,1024]{2,1,0:T(8,128)(2,1)S(1)}, u32[]{:S(2)}, u32[]{:S(2)}) collective-permute-start(bf16[1,256,1024]{2,1,0:T(8,128)(2,1)S(1)} %bitcast.186), channel_id=1, source_target_pairs={{0,1},{1,0},{2,3},{3,2},{4,5},{5,4},{6,7},{7,6},{8,9},{9,8},{10,11... | collective-permute-start | bytes 1572872 | tf_op jit(solution)/shard_map/ppermute | solution.py:806
  30.7 22.7 %collective-permute-start.2 = (bf16[1,256,1024]{2,1,0:T(8,128)(2,1)S(1)}, bf16[1,256,1024]{2,1,0:T(8,128)(2,1)S(1)}, u32[]{:S(2)}, u32[]{:S(2)}) collective-permute-start(bf16[1,256,1024]{2,1,0:T(8,128)(2,1)S(1)} %bitcast.188), channel_id=1, source_target_pairs={{0,1},{1,0},{2,3},{3,2},{4,5},{5,4},{6,7},{7,6},{8,9},{9,8},{10,11... | collective-permute-start | bytes 1572872 | tf_op jit(solution)/shard_map/ppermute | solution.py:806
  106.7 25.3 %collective-permute-start.3 = (bf16[512,1024]{1,0:T(8,128)(2,1)S(1)}, bf16[512,1024]{1,0:T(8,128)(2,1)S(1)}, u32[]{:S(2)}, u32[]{:S(2)}) collective-permute-start(bf16[512,1024]{1,0:T(8,128)(2,1)S(1)} %get-tuple-element.247), channel_id=1, source_target_pairs={{0,1},{1,0},{2,3},{3,2},{4,5},{5,4},{6,7},{7,6},{8,9},{9,8},{10,11... | collective-permute-start | bytes 3145736 | tf_op jit(solution)/shard_map/ppermute | solution.py:806
  151.5 25.6 %collective-permute-start.4 = (bf16[512,1024]{1,0:T(8,128)(2,1)}, bf16[512,1024]{1,0:T(8,128)(2,1)}, u32[]{:S(2)}, u32[]{:S(2)}) collective-permute-start(bf16[512,1024]{1,0:T(8,128)(2,1)} %get-tuple-element.251), channel_id=1, source_target_pairs={{0,1},{1,0},{2,3},{3,2},{4,5},{5,4},{6,7},{7,6},{8,9},{9,8},{10,11... | collective-permute-start | bytes 3145736 | tf_op jit(solution)/shard_map/ppermute | solution.py:806
  205.5 24.9 %collective-permute-start.5 = (bf16[512,1024]{1,0:T(8,128)(2,1)}, bf16[512,1024]{1,0:T(8,128)(2,1)}, u32[]{:S(2)}, u32[]{:S(2)}) collective-permute-start(bf16[512,1024]{1,0:T(8,128)(2,1)} %get-tuple-element.85), channel_id=1, source_target_pairs={{0,1},{1,0},{2,3},{3,2},{4,5},{5,4},{6,7},{7,6},{8,9},{9,8},{10,11... | collective-permute-start | bytes 3145736 | tf_op jit(solution)/shard_map/ppermute | solution.py:806
  292.0 17.5 %collective-permute-start.7 = (bf16[2,512,512]{2,1,0:T(8,128)(2,1)}, bf16[2,512,512]{2,1,0:T(8,128)(2,1)S(1)}, u32[]{:S(2)}, u32[]{:S(2)}) collective-permute-start(bf16[2,512,512]{2,1,0:T(8,128)(2,1)} %get-tuple-element.101), channel_id=1, source_target_pairs={{0,2},{2,0},{4,6},{6,4},{8,10},{10,8},{12,14},{14,12},{16,18},{18,... | collective-permute-start | bytes 3145736 | tf_op jit(solution)/shard_map/ppermute | solution.py:806
  292.1 17.4 %collective-permute-start.8 = (bf16[2,512,512]{2,1,0:T(8,128)(2,1)}, bf16[2,512,512]{2,1,0:T(8,128)(2,1)}, u32[]{:S(2)}, u32[]{:S(2)}) collective-permute-start(bf16[2,512,512]{2,1,0:T(8,128)(2,1)} %get-tuple-element.102), channel_id=1, source_target_pairs={{0,2},{2,0},{4,6},{6,4},{8,10},{10,8},{12,14},{14,12},{16,18},{18,... | collective-permute-start | bytes 3145736 | tf_op jit(solution)/shard_map/ppermute | solution.py:806
  298.1 11.3 %collective-permute-start.6 = (bf16[512,288]{1,0:T(8,128)(2,1)}, bf16[512,288]{1,0:T(8,128)(2,1)S(1)}, u32[]{:S(2)}, u32[]{:S(2)}) collective-permute-start(bf16[512,288]{1,0:T(8,128)(2,1)} %get-tuple-element.97), channel_id=1, source_target_pairs={{0,1},{1,0},{2,3},{3,2},{4,5},{5,4},{6,7},{7,6},{8,9},{9,8},{10,11... | collective-permute-start | bytes 884744 | tf_op jit(solution)/shard_map/ppermute | solution.py:806
  315.0 31.6 %collective-permute-start.19 = (bf16[8,64,512]{2,1,0:T(8,128)(2,1)}, bf16[8,64,512]{2,1,0:T(8,128)(2,1)}, u32[]{:S(2)}, u32[]{:S(2)}) collective-permute-start(bf16[8,64,512]{2,1,0:T(8,128)(2,1)} %get-tuple-element.129), channel_id=1, source_target_pairs={{0,4},{2,6},{4,0},{6,2},{8,12},{10,14},{12,8},{14,10},{16,20},{18,... | collective-permute-start | bytes 1572872 | tf_op jit(solution)/shard_map/ppermute | solution.py:806
  315.0 31.6 %collective-permute-start.20 = (bf16[4,128,512]{2,1,0:T(8,128)(2,1)}, bf16[4,128,512]{2,1,0:T(8,128)(2,1)}, u32[]{:S(2)}, u32[]{:S(2)}) collective-permute-start(bf16[4,128,512]{2,1,0:T(8,128)(2,1)} %get-tuple-element.131), channel_id=1, source_target_pairs={{0,8},{2,10},{4,12},{6,14},{8,0},{10,2},{12,4},{14,6},{16,24},{18,... | collective-permute-start | bytes 1572872 | tf_op jit(solution)/shard_map/ppermute | solution.py:806
  327.4 26.7 %collective-permute-start.18 = (bf16[256,1024]{1,0:T(8,128)(2,1)}, bf16[256,1024]{1,0:T(8,128)(2,1)}, u32[]{:S(2)}, u32[]{:S(2)}) collective-permute-start(bf16[256,1024]{1,0:T(8,128)(2,1)} %dynamic-slice_convert_fusion), channel_id=1, source_target_pairs={{0,1},{1,0},{2,3},{3,2},{4,5},{5,4},{6,7},{7,6},{8,9},{9,8},{10,11... | collective-permute-start | bytes 1572872 | tf_op jit(solution)/shard_map/ppermute | solution.py:806
  344.2 8.2 %collective-permute-start.9 = (bf16[8,64,312]{2,1,0:T(8,128)(2,1)S(1)}, bf16[8,64,312]{2,1,0:T(8,128)(2,1)S(1)}, u32[]{:S(2)}, u32[]{:S(2)}) collective-permute-start(bf16[8,64,312]{2,1,0:T(8,128)(2,1)S(1)} %get-tuple-element.111), channel_id=1, source_target_pairs={{0,2},{2,0},{4,6},{6,4},{8,10},{10,8},{12,14},{14,12},{16,18},{18,... | collective-permute-start | bytes 958472 | tf_op jit(solution)/shard_map/ppermute | solution.py:806
  349.6 24.4 %collective-permute-start.21 = (bf16[4,64,512]{2,1,0:T(8,128)(2,1)S(1)}, bf16[4,64,512]{2,1,0:T(8,128)(2,1)S(1)}, u32[]{:S(2)}, u32[]{:S(2)}) collective-permute-start(bf16[4,64,512]{2,1,0:T(8,128)(2,1)S(1)} %get-tuple-element.133), channel_id=1, source_target_pairs={{0,8},{2,10},{4,12},{6,14},{8,0},{10,2},{12,4},{14,6},{16,24},{18,... | collective-permute-start | bytes 786440 | tf_op jit(solution)/shard_map/ppermute | solution.py:806
  351.0 23.1 %collective-permute-start.22 = (bf16[2,128,512]{2,1,0:T(8,128)(2,1)S(1)}, bf16[2,128,512]{2,1,0:T(8,128)(2,1)S(1)}, u32[]{:S(2)}, u32[]{:S(2)}) collective-permute-start(bf16[2,128,512]{2,1,0:T(8,128)(2,1)S(1)} %get-tuple-element.135), channel_id=1, source_target_pairs={{0,16},{2,18},{4,20},{6,22},{8,24},{10,26},{12,28},{14,30},{16,0},... | collective-permute-start | bytes 786440 | tf_op jit(solution)/shard_map/ppermute | solution.py:806
  359.3 6.7 %collective-permute-start.11 = (bf16[2,64,312]{2,1,0:T(8,128)(2,1)S(1)}, bf16[2,64,312]{2,1,0:T(8,128)(2,1)S(1)}, u32[]{:S(2)}, u32[]{:S(2)}) collective-permute-start(bf16[2,64,312]{2,1,0:T(8,128)(2,1)S(1)} %get-tuple-element.115), channel_id=1, source_target_pairs={{0,8},{2,10},{4,12},{6,14},{8,0},{10,2},{12,4},{14,6},{16,24},{18,... | collective-permute-start | bytes 239624 | tf_op jit(solution)/shard_map/ppermute | solution.py:806
  371.1 6.9 %collective-permute-start.13 = (bf16[1,1,64,312]{3,2,1,0:T(8,128)(2,1)S(1)}, bf16[1,1,64,312]{3,2,1,0:T(8,128)(2,1)S(1)}, u32[]{:S(2)}, u32[]{:S(2)}) collective-permute-start(bf16[1,1,64,312]{3,2,1,0:T(8,128)(2,1)S(1)} %get-tuple-element.219), channel_id=1, source_target_pairs={{0,1},{1,0},{2,3},{3,2},{4,5},{5,4},{6,7},{7,6},{8,9},{9,8},{10,11... | collective-permute-start | bytes 119816 | tf_op jit(solution)/shard_map/ppermute | solution.py:806
  375.1 11.2 %collective-permute-start.23 = (bf16[2,64,512]{2,1,0:T(8,128)(2,1)S(1)}, bf16[2,64,512]{2,1,0:T(8,128)(2,1)S(1)}, u32[]{:S(2)}, u32[]{:S(2)}) collective-permute-start(bf16[2,64,512]{2,1,0:T(8,128)(2,1)S(1)} %get-tuple-element.137), channel_id=1, source_target_pairs={{0,16},{2,18},{4,20},{6,22},{8,24},{10,26},{12,28},{14,30},{16,0},... | collective-permute-start | bytes 393224 | tf_op jit(solution)/shard_map/ppermute | solution.py:806
  376.6 17.4 %collective-permute-start.24 = (bf16[2,64,512]{2,1,0:T(8,128)(2,1)S(1)}, bf16[2,64,512]{2,1,0:T(8,128)(2,1)S(1)}, u32[]{:S(2)}, u32[]{:S(2)}) collective-permute-start(bf16[2,64,512]{2,1,0:T(8,128)(2,1)S(1)} %get-tuple-element.139), channel_id=1, source_target_pairs={{0,4},{2,6},{4,0},{6,2},{8,12},{10,14},{12,8},{14,10},{16,20},{18,... | collective-permute-start | bytes 393224 | tf_op jit(solution)/shard_map/ppermute | solution.py:806
  378.0 8.1 %collective-permute-start.14 = (bf16[1,1,1,1,1,2,64,312]{7,6,5,4,3,2,1,0:T(8,128)(2,1)S(1)}, bf16[1,1,1,1,1,2,64,312]{7,6,5,4,3,2,1,0:T(8,128)(2,1)S(1)}, u32[]{:S(2)}, u32[]{:S(2)}) collective-permute-start(bf16[1,1,1,1,1,2,64,312]{7,6,5,4,3,2,1,0:T(8,128)(2,1)S(1)} %maximum_select_fusion.9), channel_id=1, source_target_pairs={{0,16},{2,18},{4,20},{6,22},{8,24},{10,26},{12,28},{14,30},{16,0},... | collective-permute-start | bytes 239624 | tf_op jit(solution)/shard_map/ppermute | solution.py:806
  392.1 8.7 %collective-permute-start.16 = (bf16[2,2,1,1,1,2,64,312]{7,6,5,0,1,4,3,2:T(8,128)(2,1)S(1)}, bf16[2,2,1,1,1,2,64,312]{7,6,5,0,1,4,3,2:T(8,128)(2,1)S(1)}, u32[]{:S(2)}, u32[]{:S(2)}) collective-permute-start(bf16[2,2,1,1,1,2,64,312]{7,6,5,0,1,4,3,2:T(8,128)(2,1)S(1)} %maximum_select_fusion.5), channel_id=1, source_target_pairs={{0,4},{2,6},{4,0},{6,2},{8,12},{10,14},{12,8},{14,10},{16,20},{18,... | collective-permute-start | bytes 958472 | tf_op jit(solution)/shard_map/ppermute | solution.py:806
  (107 other events, 983.1 us)
Sparse Core Ops, SparseCore 0:
  10.9 53.2 all-gather.2
  66.9 73.3 all-gather.4
  205.6 102.9 reduce-scatter.1
